TPU v7x, 128 devices: a whole 4x4x4 slice. The times are simulated.
128 devices in a mesh: owner: 32 (over x, z, core), view: 4 (over y).
Axes of the slice: x: 4, y: 4, z: 4, core: 2. Of those that a mesh axis runs over, the one named last changes fastest.
Arguments:
- estimate: float32 [512, 128, 512], P('owner'), may hold values from 0.5 to 2
- axial_views: float32 [4, 512, 128, 512], P('view', 'owner'), may hold values from 0.3 to 3
- lateral_views: float32 [4, 512, 128, 512], P('view', 'owner'), may hold values from 0.3 to 3
- psf_axial: float32 [4, 3, 33], P('view'), may hold values from 0.05 to 1
- psf_lateral: float32 [4, 3, 33], P('view'), may hold values from 0.05 to 1
- coverage: int32 [32, 4, 8], P('owner'), may hold values from 0 to 1, as said below
Outputs:
- deconvolved: float32 [512, 128, 512], P('owner')
Inputs may be any that keep to these rules, and one draw needn't show every extreme that they name: `coverage`: each block is covered by 2 to 6 views; some block by exactly 6 and some by exactly 2.
All inputs are finite; a program needn't handle non-finite values.
Results may differ from a plain program's by a relative error of at most 0.0001.
Values sent between devices are 32-bit elements; how exact they have to be, the bound alone decides.
No kernel may reach another device: no remote copies, remote signals or barrier semaphores. Data moves between devices by JAX's collectives and lax.ppermute only.
A program may use at most 128 MiB of HBM per device.

v0:
```python
import jax
import jax.numpy as jnp
from jax import lax
from jax.experimental import pallas as pl
from jax.experimental.pallas import tpu as pltpu
from jax.sharding import PartitionSpec as P


ITERS = 2
VA = 4
RIM = 16
UNROLL = 4
BF = jnp.bfloat16
F32 = jnp.float32

COLS = 8
GROUPS = [list(range(8 * g, 8 * g + 8)) for g in range(4)]
Z_UP = [(8 * x + k, 8 * x + 8 + k) for x in range(3) for k in range(8)]
Z_DOWN = [(b, a) for a, b in Z_UP]
X_UP = [(8 * x + k, 8 * x + k + 1) for x in range(4) for k in range(7)]
X_DOWN = [(b, a) for a, b in X_UP]
V_UP = [(i, (i + 1) % 4) for i in range(4)]
V_DOWN = [(b, a) for a, b in V_UP]


def axial_round(d):
    return [(8 * x + k, 8 * x + (k + d) % 8) for x in range(4) for k in range(8)]


def lateral_round(t):
    return [
        (4 * k + r, ((r + t + k // 2) % 4) * 8 + k) for k in range(8) for r in range(4)
    ]


def split(value):
    hi = value.astype(BF)
    lo = (value - hi.astype(F32)).astype(BF)
    return hi, lo


def band(kernel, length, extended):
    rim = RIM if extended else 0
    taps = kernel.shape[-1]
    row = jnp.arange(length)[:, None]
    col = jnp.arange(length + 2 * rim)[None, :]
    offset = col - row + (RIM - rim)
    hit = offset[:, :, None] == jnp.arange(taps)[None, None, :]
    return jnp.sum(jnp.where(hit, kernel[..., None, None, :], 0.0), axis=-1)


def edge_weights(kernel, positions, total):
    source = positions[:, None] + jnp.arange(kernel.shape[-1])[None, :] - RIM
    inside = (source >= 0) & (source < total)
    return jnp.sum(jnp.where(inside, kernel[..., None, :], 0.0), axis=-1)


def split_matrix(value):
    hi = lax.reduce_precision(value, 8, 7)
    return hi.astype(BF), (value - hi).astype(BF)


def left_form(matrix):
    hi, lo = split_matrix(matrix)
    return jnp.concatenate([hi, lo, hi], axis=-1)


def right_form(matrix):
    hi, lo = split_matrix(matrix)
    top = jnp.concatenate([hi, lo], axis=-1)
    low = jnp.concatenate([hi, jnp.zeros_like(lo)], axis=-1)
    return jnp.concatenate([top, low], axis=-2)


def dot(a, b):
    return lax.dot_general(a, b, (((1,), (0,)), ((), ())), preferred_element_type=F32)


def conv_rows(matrix, data):
    hi, lo = split(data)
    return dot(matrix, jnp.concatenate([hi, hi, lo], axis=0))


def conv_lanes(data, matrix):
    hi, lo = split(data)
    both = dot(jnp.concatenate([hi, lo], axis=1), matrix)
    half = data.shape[1]
    return both[:, :half] + both[:, half:]


def xy_planes(load, mx, my, planes, mid_ref, finish):
    group = 2 * UNROLL
    steps = planes // group

    def along_x(i):
        for u in range(0, group, 2):
            p = group * i + u
            mid = conv_rows(mx, jnp.concatenate([load(p), load(p + 1)], axis=1))
            half = mid.shape[0]
            slot = lax.rem(i, 2)
            mid_ref[slot, u * half : (u + 1) * half] = mid[:, :128]
            mid_ref[slot, (u + 1) * half : (u + 2) * half] = mid[:, 128:]

    def along_y(i):
        done = conv_lanes(mid_ref[lax.rem(i, 2)], my)
        half = done.shape[0] // group
        for u in range(group):
            finish(group * i + u, done[u * half : (u + 1) * half])

    def body(i, _):
        along_y(i - 1)
        along_x(i)
        return 0

    along_x(0)
    lax.fori_loop(1, steps, body, 0)
    along_y(steps - 1)


def z_columns(load, mz, columns, store):
    def body(i, _):
        for u in range(UNROLL):
            x = 2 * (UNROLL * i + u)
            out = conv_rows(mz, jnp.concatenate([load(x), load(x + 1)], axis=1))
            store(x, out[:, :128])
            store(x + 1, out[:, 128:])
        return 0

    lax.fori_loop(0, columns // (2 * UNROLL), body, 0)


def each(count, step):
    def body(i, _):
        for u in range(UNROLL):
            step(UNROLL * i + u)
        return 0

    lax.fori_loop(0, count // UNROLL, body, 0)


def forward_kernel(
    mz_ref, mx_ref, my_ref, f_ref, zb_ref, za_ref, xl_ref, xr_ref, cl_ref, cr_ref, obs_ref,
    q_ref, first_ref, last_ref, e_ref, w_ref, mid_ref,
):
    depth, width = f_ref.shape[0], f_ref.shape[1]
    wide = width + 2 * RIM
    pitch = wide + 1
    part = width + 1
    mz = mz_ref[...]

    def middle(source, start):
        def step(z):
            e_ref[pl.ds((start + z) * pitch + RIM, width), :] = source[z]

        each(source.shape[0], step)

    def edge(z, left, right):
        e_ref[pl.ds(z * pitch, RIM), :] = left
        e_ref[pl.ds(z * pitch + RIM + width, RIM), :] = right

    def sides(z):
        edge(RIM + z, xl_ref[z], xr_ref[z])

    def corners(z):
        edge(z, cl_ref[z], cr_ref[z])
        edge(RIM + depth + z, cl_ref[RIM + z], cr_ref[RIM + z])

    middle(zb_ref, 0)
    middle(f_ref, RIM)
    middle(za_ref, RIM + depth)
    each(depth, sides)
    each(RIM, corners)

    def load(x):
        return e_ref[pl.ds(x, depth + 2 * RIM, stride=pitch), :]

    def store(x, value):
        w_ref[pl.ds(x, depth, stride=pitch), :] = value

    z_columns(load, mz, wide, store)

    def finish(p, blurred):
        q_ref[pl.ds(p * part, width), :] = obs_ref[p] / blurred

    xy_planes(
        lambda p: w_ref[pl.ds(p * pitch, wide), :], mx_ref[...], my_ref[...], depth, mid_ref, finish
    )

    def edges(z):
        first_ref[z] = q_ref[pl.ds(z * part, width), :]
        last_ref[z] = q_ref[pl.ds((depth - RIM + z) * part, width), :]

    each(RIM, edges)


def back_z_kernel(mz_ref, q_ref, zb_ref, za_ref, r_ref, first_ref, last_ref, b_ref, a_ref):
    width = zb_ref.shape[1]
    part = width + 1
    depth = q_ref.shape[0] // part

    def rims(z):
        b_ref[pl.ds(z * part, width), :] = zb_ref[z]
        a_ref[pl.ds(z * part, width), :] = za_ref[z]

    each(RIM, rims)

    def load(x):
        return jnp.concatenate(
            [
                b_ref[pl.ds(x, RIM, stride=part), :],
                q_ref[pl.ds(x, depth, stride=part), :],
                a_ref[pl.ds(x, RIM, stride=part), :],
            ],
            axis=0,
        )

    def store(x, value):
        r_ref[pl.ds(x, depth, stride=part), :] = value

    z_columns(load, mz_ref[...], width, store)

    def edges(z):
        first_ref[z] = r_ref[pl.ds(z * part, RIM), :]
        last_ref[z] = r_ref[pl.ds(z * part + width - RIM, RIM), :]

    each(depth, edges)


def back_xy_kernel(me_ref, w_ref, mx_ref, my_ref, r_ref, xl_ref, xr_ref, *rest):
    acc_ref, l_ref, mid_ref = rest if len(rest) == 3 else (None, *rest)
    me = me_ref[0]
    depth = xl_ref.shape[0]
    part = r_ref.shape[0] // depth

    def load(p):
        return jnp.concatenate(
            [xl_ref[p], r_ref[pl.ds(p * part, part - 1), :], xr_ref[p]], axis=0
        )

    def finish(p, back):
        term = w_ref[lax.div(p, 16)] * jnp.log(back)
        for quarter in range(4):
            slot = lax.rem(quarter - me + 4, 4)
            piece = term[quarter * 16 : quarter * 16 + 16]
            if acc_ref is not None:
                piece = piece + acc_ref[slot, p]
            l_ref[slot, p] = piece

    xy_planes(load, mx_ref[...], my_ref[...], depth, mid_ref, finish)


def assemble_kernel(at_ref, *refs):
    *pieces, block_ref, first_ref, last_ref, low_ref, high_ref = refs
    depth, narrow = pieces[0].shape[0], pieces[0].shape[1]
    for number, piece in enumerate(pieces):
        at = pl.multiple_of(at_ref[number], narrow)

        def step(z):
            block_ref[z, pl.ds(at, narrow), :] = piece[z]

        each(depth, step)
    first_ref[...] = block_ref[:RIM]
    last_ref[...] = block_ref[depth - RIM :]
    width = block_ref.shape[1]
    low_ref[...] = block_ref[:, :RIM]
    high_ref[...] = block_ref[:, width - RIM :]


def stack_kernel(at_ref, *refs):
    *pieces, block_ref = refs
    for number, piece in enumerate(pieces):
        block_ref[pl.ds(at_ref[number], piece.shape[0])] = piece[...]


def turn_kernel(at_ref, *refs):
    *pieces, out_ref, rows_ref = refs
    slab, columns = out_ref.shape[0], out_ref.shape[2]
    narrow = pieces[0].shape[1]
    width = narrow * len(pieces)
    count = columns // width
    starts = [pl.multiple_of(at_ref[number], narrow) for number in range(len(pieces))]

    def step(z, _):
        for number, piece in enumerate(pieces):
            for g in range(count):
                rows_ref[pl.ds(g * width + starts[number], narrow), :] = piece[z * count + g]
        out_ref[z] = rows_ref[...].T
        return 0

    lax.fori_loop(0, slab, step, 0)


VMEM = pl.BlockSpec(memory_space=pltpu.VMEM)
SMEM = pl.BlockSpec(memory_space=pltpu.SMEM)


def params(mebibytes):
    return pltpu.CompilerParams(vmem_limit_bytes=mebibytes * 2**20)


def forward(mz, mx, my, f, zb, za, xl, xr, cl, cr, obs):
    depth, width, lines = f.shape
    rim = jax.ShapeDtypeStruct((RIM, width, lines), F32)
    pitch = width + 2 * RIM + 1
    return pl.pallas_call(
        forward_kernel,
        in_specs=[VMEM] * 11,
        out_specs=[VMEM] * 3,
        out_shape=[jax.ShapeDtypeStruct((depth * (width + 1), lines), F32), rim, rim],
        scratch_shapes=[
            pltpu.VMEM(((depth + 2 * RIM) * pitch, lines), F32),
            pltpu.VMEM((depth * pitch, lines), F32),
            pltpu.VMEM((2, 2 * UNROLL * width, lines), F32),
        ],
        compiler_params=params(20),
        cost_estimate=pl.CostEstimate(flops=10**10, bytes_accessed=2 * 10**7, transcendentals=0),
        name="forward",
    )(mz, mx, my, f, zb, za, xl, xr, cl, cr, obs)


def back_z(mz, q, zb, za):
    width, lines = zb.shape[1:]
    depth = q.shape[0] // (width + 1)
    rim = jax.ShapeDtypeStruct((depth, RIM, lines), F32)
    padded = pltpu.VMEM((RIM * (width + 1), lines), F32)
    return pl.pallas_call(
        back_z_kernel,
        in_specs=[VMEM] * 4,
        out_specs=[VMEM] * 3,
        out_shape=[jax.ShapeDtypeStruct(q.shape, F32), rim, rim],
        scratch_shapes=[padded, padded],
        compiler_params=params(12),
        cost_estimate=pl.CostEstimate(flops=3 * 10**9, bytes_accessed=10**7, transcendentals=0),
        name="back_z",
    )(mz, q, zb, za)


def back_xy(me, weight, mx, my, r, xl, xr, acc=None):
    depth, _, lines = xl.shape
    width = r.shape[0] // depth - 1
    args = [me, weight, mx, my, r, xl, xr] + ([] if acc is None else [acc])
    return pl.pallas_call(
        back_xy_kernel,
        in_specs=[SMEM, SMEM] + [VMEM] * (len(args) - 2),
        out_specs=VMEM,
        out_shape=jax.ShapeDtypeStruct((4, depth, width // 4, lines), F32),
        scratch_shapes=[pltpu.VMEM((2, 2 * UNROLL * width, lines), F32)],
        compiler_params=params(12),
        cost_estimate=pl.CostEstimate(flops=5 * 10**9, bytes_accessed=10**7, transcendentals=10**6),
        name="back_xy",
    )(*args)


def assemble(at, pieces):
    depth, narrow, lines = pieces[0].shape
    width = narrow * len(pieces)
    rim = jax.ShapeDtypeStruct((RIM, width, lines), F32)
    side = jax.ShapeDtypeStruct((depth, RIM, lines), F32)
    return pl.pallas_call(
        assemble_kernel,
        in_specs=[SMEM] + [VMEM] * len(pieces),
        out_specs=[VMEM] * 5,
        out_shape=[jax.ShapeDtypeStruct((depth, width, lines), F32), rim, rim, side, side],
        compiler_params=params(16),
        cost_estimate=pl.CostEstimate(flops=10**6, bytes_accessed=10**7, transcendentals=0),
        name="assemble",
    )(at.astype(jnp.int32), *pieces)


def stack(at, pieces):
    slab, width, lines = pieces[0].shape
    return pl.pallas_call(
        stack_kernel,
        in_specs=[SMEM] + [VMEM] * len(pieces),
        out_specs=VMEM,
        out_shape=jax.ShapeDtypeStruct((slab * len(pieces), width, lines), F32),
        compiler_params=params(16),
        cost_estimate=pl.CostEstimate(flops=10**6, bytes_accessed=10**7, transcendentals=0),
        name="stack",
    )(at.astype(jnp.int32), *pieces)


def turn(at, pieces, slab):
    rows, narrow, lines = pieces[0].shape
    columns = rows // slab * narrow * len(pieces)
    return pl.pallas_call(
        turn_kernel,
        in_specs=[SMEM] + [VMEM] * len(pieces),
        out_specs=VMEM,
        out_shape=jax.ShapeDtypeStruct((slab, lines, columns), F32),
        scratch_shapes=[pltpu.VMEM((columns, lines), F32)],
        compiler_params=params(16),
        name="turn",
    )(at.astype(jnp.int32), *pieces)


def gather_quarters(quarter, half):
    below = lax.ppermute(quarter, "view", V_UP)
    above = lax.ppermute(quarter, "view", V_DOWN)
    first = lax.ppermute(below[:half], "view", V_UP)
    second = lax.ppermute(above[half:], "view", V_DOWN)
    return quarter, above, jnp.concatenate([first, second], axis=0), below


def scatter_quarters(parts):
    half = parts.shape[1] // 2
    first = lax.ppermute(parts[2, :half], "view", V_UP)
    second = lax.ppermute(parts[2, half:], "view", V_DOWN)
    up = jnp.concatenate([parts[1, :half] + first, parts[1, half:]], axis=0)
    down = jnp.concatenate([parts[3, :half], parts[3, half:] + second], axis=0)
    return parts[0] + lax.ppermute(up, "view", V_UP) + lax.ppermute(down, "view", V_DOWN)


def to_blocks(value):
    return lax.all_to_all(
        value, "owner", split_axis=1, concat_axis=0, axis_index_groups=GROUPS, tiled=True
    )


def z_rims(first, last):
    before = lax.ppermute(last, "owner", Z_UP)
    after = lax.ppermute(first, "owner", Z_DOWN)
    return before, after


def x_rims(first, last):
    left = lax.ppermute(last, "owner", X_UP)
    right = lax.ppermute(first, "owner", X_DOWN)
    return left, right


def local(estimate, axial_views, lateral_views, psf_axial, psf_lateral, coverage):
    slab, lines, columns = estimate.shape
    owner = lax.axis_index("owner")
    me = lax.axis_index("view")
    k = owner % 8
    z_chip = owner // 8
    width = columns // COLS
    depth = 8 * slab

    turned = estimate.transpose(0, 2, 1).reshape(slab, COLS, 4, width // 4, lines)
    mine = lax.dynamic_index_in_dim(turned, me, 2, keepdims=False)
    cover = jnp.repeat(coverage[0].astype(F32), 2, axis=0)
    cover = jnp.pad(cover[:, None, :], ((0, 0), (0, width // 4 - 1), (0, lines - cover.shape[1])))
    mine = jnp.concatenate([mine, cover[None]], axis=0).reshape(slab + 1, -1, lines)
    lateral_views, mine = lax.optimization_barrier((lateral_views, mine))
    got = to_blocks(mine).reshape(8, slab + 1, width // 4, lines)

    chunks = lateral_views[0].transpose(2, 0, 1).reshape(4, depth, slab, lines)
    pieces, places = [], []
    for t in range(4):
        target = (owner % 4 + t + z_chip) % 4
        pieces.append(lax.dynamic_index_in_dim(chunks, target, 0, keepdims=False))
        places.append(((z_chip - t - k // 2) % 4) * slab)
    axial_views, got, *pieces = lax.optimization_barrier((axial_views, got, *pieces))
    quarter = got[:, :slab].reshape(depth, width // 4, lines)
    cover = got[:, slab, 0, :8]
    pieces = [
        lax.ppermute(piece, "owner", lateral_round(t)) for t, piece in enumerate(pieces)
    ]
    axial_chunks = axial_views[0].transpose(0, 2, 1).reshape(slab, COLS, width, lines)
    axial_chunks = axial_chunks.transpose(1, 0, 2, 3)
    slabs = [
        lax.dynamic_index_in_dim(axial_chunks, (k + d) % 8, 0, keepdims=False) for d in range(8)
    ]
    slabs = [
        lax.ppermute(piece, "owner", axial_round(d)) if d else piece
        for d, piece in enumerate(slabs)
    ]
    axial = stack((k - jnp.arange(8)) % 8 * slab, slabs)
    lateral = assemble(jnp.stack(places), pieces)[0]

    count = jnp.sum(cover, axis=-1)
    weight_axial = lax.dynamic_index_in_dim(cover, me, 1, keepdims=False)
    weight_lateral = lax.dynamic_index_in_dim(cover, VA + me, 1, keepdims=False)

    taps = jnp.concatenate([psf_axial, psf_lateral], axis=0)
    taps = taps / jnp.sum(taps, axis=-1, keepdims=True)
    flipped = taps[..., ::-1]
    z_at = z_chip * depth + jnp.arange(depth)
    x_at = k * width + jnp.arange(width)
    y_at = jnp.arange(lines)
    ahead_z = left_form(band(taps[:, 0], depth, True))
    ahead_x = left_form(band(taps[:, 2], width, True))
    ahead_y = right_form(jnp.swapaxes(band(taps[:, 1], lines, False), 1, 2))
    wz = edge_weights(flipped[:, 0], z_at, 4 * depth)
    wx = edge_weights(flipped[:, 2], x_at, columns)
    wy = edge_weights(flipped[:, 1], y_at, lines)
    back_mz = left_form(band(flipped[:, 0], depth, True) / wz[:, :, None])
    back_mx = left_form(band(flipped[:, 2], width, True) / wx[:, :, None])
    back_my = right_form(
        jnp.swapaxes(band(flipped[:, 1], lines, False) / wy[:, :, None], 1, 2)
    )
    me_arr = me[None].astype(jnp.int32)

    for _ in range(ITERS):
        pieces = gather_quarters(quarter, depth // 2)
        places = ((me + jnp.arange(4)) % 4) * (width // 4)
        block, first, last, low, high = assemble(places, pieces)
        before, after = z_rims(first, last)
        left, right = x_rims(low, high)
        corner_left, corner_right = x_rims(
            jnp.concatenate([before[:, :RIM], after[:, :RIM]], axis=0),
            jnp.concatenate([before[:, -RIM:], after[:, -RIM:]], axis=0),
        )
        logs = None
        for number, (obs, weight) in [*enumerate(
            ((axial, weight_axial), (lateral, weight_lateral))
        )][::-1]:
            quotient, first, last = forward(
                ahead_z[number], ahead_x[number], ahead_y[number],
                block, before, after, left, right, corner_left, corner_right, obs,
            )
            rz, low, high = back_z(back_mz[number], quotient, *z_rims(first, last))
            logs = back_xy(
                me_arr, weight, back_mx[number], back_my[number],
                rz, *x_rims(low, high), acc=logs,
            )
        total = scatter_quarters(logs)
        slabs = total.reshape(8, slab, width // 4, lines) / count[:, None, None, None]
        quarter = quarter * jnp.exp(slabs.reshape(quarter.shape))

    slabs = lax.all_to_all(
        quarter, "owner", split_axis=0, concat_axis=1, axis_index_groups=GROUPS, tiled=True
    )
    pieces = gather_quarters(slabs, slab // 2)
    pieces = [piece.reshape(slab * COLS, width // 4, lines) for piece in pieces]
    return turn(((me + jnp.arange(4)) % 4) * (width // 4), pieces, slab)


def solution(mesh):
    in_specs = (
        P("owner", None, None),
        P("view", "owner", None, None),
        P("view", "owner", None, None),
        P("view", None, None),
        P("view", None, None),
        P("owner", None, None),
    )
    out_specs = P("owner", None, None)
    return jax.shard_map(local, mesh=mesh, in_specs=in_specs, out_specs=out_specs, check_vma=False)
```

profile of v0, /device:TPU:1, one launch (start us, length us, event | category | flops | bytes accessed | tf_op | source)
XLA Modules:
  0.0 572.9 jit_solution(17765761012405298660)
XLA Ops:
  0.0 5.3 copy.69
  8.6 6.8 %all-to-all-start = ((f32[17,128,128]{2,0,1:T(8,128)}), f32[17,128,128]{2,0,1:T(8,128)S(1)}, u32[]{:S(2)}, u32[]{:S(2)}) async-start(f32[17,128,128]{2,0,1:T(8,128)} %copy.71), calls=%async_computation | async-start | bytes 3145728 | tf_op jit(solution)/shard_map/all_to_all | solution.py:415
  19.9 5.4 copy.90
  28.3 4.3 dynamic-slice_bitcast_fusion
  46.7 5.3 copy.88
  52.0 4.3 dynamic-slice_bitcast_fusion.4
  64.0 2.7 collective-permute-start.3
  71.1 13.2 %collective-permute-done.11.refs_2_ = f32[16,64,128]{2,1,0:T(8,128)} collective-permute-done((f32[16,64,128]{2,1,0:T(8,128)}, f32[16,64,128]{2,1,0:T(8,128)}, u32[]{:S(2)}, u32[]{:S(2)}) %collective-permute-start.11) | collective-permute-done | bytes 524320 | tf_op jit(solution)/shard_map/ppermute | solution.py:467
  85.2 14.4 %collective-permute-done.12.refs_3_ = f32[16,64,128]{2,1,0:T(8,128)} collective-permute-done((f32[16,64,128]{2,1,0:T(8,128)}, f32[16,64,128]{2,1,0:T(8,128)}, u32[]{:S(2)}, u32[]{:S(2)}) %collective-permute-start.12) | collective-permute-done | bytes 524320 | tf_op jit(solution)/shard_map/ppermute | solution.py:467
  103.3 12.0 %collective-permute-start.15 = (f32[16,64,128]{2,1,0:T(8,128)}, f32[16,64,128]{2,1,0:T(8,128)}, u32[]{:S(2)}, u32[]{:S(2)}) collective-permute-start(f32[16,64,128]{2,1,0:T(8,128)} %get-tuple-element.112), channel_id=1, source_target_pairs={{0,24},{4,28},{8,0},{12,4},{16,8},{20,12},{24,16},{28,20},{32,56},... | collective-permute-start | bytes 1572872 | tf_op jit(solution)/shard_map/ppermute | solution.py:467
  123.2 10.9 %collective-permute-done.15.refs_6_ = f32[16,64,128]{2,1,0:T(8,128)} collective-permute-done((f32[16,64,128]{2,1,0:T(8,128)}, f32[16,64,128]{2,1,0:T(8,128)}, u32[]{:S(2)}, u32[]{:S(2)}) %collective-permute-start.15) | collective-permute-done | bytes 524320 | tf_op jit(solution)/shard_map/ppermute | solution.py:467
  134.1 7.0 %collective-permute-start.22 = (f32[128,16,128]{2,1,0:T(8,128)S(1)}, f32[128,16,128]{2,1,0:T(8,128)S(1)}, u32[]{:S(2)}, u32[]{:S(2)}) collective-permute-start(f32[128,16,128]{2,1,0:T(8,128)S(1)} %copy-done.12), channel_id=1, source_target_pairs={{0,32},{4,64},{8,96},{12,0},{16,36},{20,68},{24,100},{28,4},{32,72... | collective-permute-start | bytes 3145736 | tf_op jit(solution)/shard_map/ppermute | solution.py:459
  141.1 3.2 collective-permute-start.23
  146.4 4.0 collective-permute-start.6
  152.5 11.7 %collective-permute-done.22.refs_1_ = f32[128,16,128]{2,1,0:T(8,128)S(1)} collective-permute-done((f32[128,16,128]{2,1,0:T(8,128)S(1)}, f32[128,16,128]{2,1,0:T(8,128)S(1)}, u32[]{:S(2)}, u32[]{:S(2)}) %collective-permute-start.22) | collective-permute-done | bytes 1048608 | tf_op jit(solution)/shard_map/ppermute | solution.py:459
  166.1 18.2 %collective-permute-done.23.refs_2_ = f32[128,16,128]{2,1,0:T(8,128)S(1)} collective-permute-done((f32[128,16,128]{2,1,0:T(8,128)S(1)}, f32[128,16,128]{2,1,0:T(8,128)S(1)}, u32[]{:S(2)}, u32[]{:S(2)}) %collective-permute-start.23) | collective-permute-done | bytes 1048608 | tf_op jit(solution)/shard_map/ppermute | solution.py:459
  184.3 15.9 %collective-permute-start.8 = (f32[32,16,128]{2,1,0:T(8,128)S(1)}, f32[32,16,128]{2,1,0:T(8,128)S(1)}, u32[]{:S(2)}, u32[]{:S(2)}) collective-permute-start(f32[32,16,128]{2,1,0:T(8,128)S(1)} %pad_maximum_fusion.10), channel_id=1, source_target_pairs={{0,4},{4,8},{8,12},{12,16},{16,20},{20,24},{24,28},{32,36},{36,40}... | collective-permute-start | bytes 786440 | tf_op jit(solution)/shard_map/ppermute | solution.py:427
  200.3 2.3 stack.21.obs_ref
  202.6 4.8 assemble.4
  207.4 10.6 %forward.5 = (f32[8320,128]{1,0:T(8,128)S(1)}, f32[16,64,128]{2,1,0:T(8,128)S(1)}, f32[16,64,128]{2,1,0:T(8,128)S(1)}) custom-call(bf16[128,480]{1,0:T(8,128)(2,1)S(1)} %get-tuple-element.135.mz_ref, bf16[64,288]{1,0:T(8,128)(2,1)S(1)} %get-tuple-element.149.mx_ref, bf16[256,256]{1,0:T(8,128)(2,1)S(1)} %get-tuple-element.133.my_ref, ...), custom_call_target="tpu_custom_call" | custom-call | flops 10000000000 | bytes 20000000 | tf_op jit(solution)/shard_map/forward/pallas_call | solution.py:305
  220.7 10.6 %forward.4 = (f32[8320,128]{1,0:T(8,128)S(1)}, f32[16,64,128]{2,1,0:T(8,128)S(1)}, f32[16,64,128]{2,1,0:T(8,128)S(1)}) custom-call(bf16[128,480]{1,0:T(8,128)(2,1)S(1)} %get-tuple-element.136.mz_ref, bf16[64,288]{1,0:T(8,128)(2,1)S(1)} %get-tuple-element.150.mx_ref, bf16[256,256]{1,0:T(8,128)(2,1)S(1)} %get-tuple-element.134.my_ref, ...), custom_call_target="tpu_custom_call" | custom-call | flops 10000000000 | bytes 20000000 | tf_op jit(solution)/shard_map/forward/pallas_call | solution.py:305
  231.3 4.0 collective-permute-start.17
  236.8 4.4 back_z.5
  243.3 3.2 collective-permute-start.27
  246.5 2.2 collective-permute-start.28
  250.4 4.5 back_z.4
  258.8 3.4 collective-permute-start.20
  263.7 2.2 copy-done.8
  265.9 7.1 %back_xy.4.rest_0_ = f32[4,128,16,128]{3,2,1,0:T(8,128)S(1)} custom-call(s32[1]{0:T(128)} %bitcast.17.me_ref, f32[8]{0:T(128)S(1)} %get-tuple-element.97.w_ref, bf16[64,288]{1,0:T(8,128)(2,1)S(1)} %get-tuple-element.151.mx_ref, bf16[256,256]{1,0:T(8,128)(2,1)S(1)} %get-tuple-element.139.my_ref, f32[8320,128]{1,0:T(8,128)S(1)} %copy-done.8, ...), custom_call_target="tpu_custom_call" | custom-call | flops 5000000000 | bytes 10000000 | tf_op jit(solution)/shard_map/back_xy/pallas_call | solution.py:342
  273.0 2.2 collective-permute-done.20.xr_ref
  275.2 7.1 %back_xy.5 = f32[4,128,16,128]{3,2,1,0:T(8,128)S(1)} custom-call(s32[1]{0:T(128)} %bitcast.17.me_ref, f32[8]{0:T(128)S(1)} %get-tuple-element.98.w_ref, bf16[64,288]{1,0:T(8,128)(2,1)S(1)} %get-tuple-element.152.mx_ref, bf16[256,256]{1,0:T(8,128)(2,1)S(1)} %get-tuple-element.140.my_ref, f32[8320,128]{1,0:T(8,128)S(1)} %bitcast.167, ...), custom_call_target="tpu_custom_call" | custom-call | flops 5000000000 | bytes 10000000 | tf_op jit(solution)/shard_map/back_xy/pallas_call | solution.py:342
  282.7 2.6 collective-permute-start.31
  285.3 9.9 %collective-permute-done.29 = f32[64,16,128]{2,1,0:T(8,128)S(1)} collective-permute-done((f32[64,16,128]{2,1,0:T(8,128)S(1)}, f32[64,16,128]{2,1,0:T(8,128)S(1)}, u32[]{:S(2)}, u32[]{:S(2)}) %collective-permute-start.29) | collective-permute-done | bytes 524320 | tf_op jit(solution)/shard_map/ppermute | solution.py:407
  296.9 2.5 collective-permute-start.32
  299.6 21.1 %collective-permute-done.30 = f32[128,16,128]{2,1,0:T(8,128)} collective-permute-done((f32[128,16,128]{2,1,0:T(8,128)S(1)}, f32[128,16,128]{2,1,0:T(8,128)}, u32[]{:S(2)}, u32[]{:S(2)}) %collective-permute-start.30) | collective-permute-done | bytes 1048608 | tf_op jit(solution)/shard_map/ppermute | solution.py:411
  327.3 23.6 %collective-permute-done.34.refs_3_ = f32[128,16,128]{2,1,0:T(8,128)S(1)} collective-permute-done((f32[128,16,128]{2,1,0:T(8,128)S(1)}, f32[128,16,128]{2,1,0:T(8,128)S(1)}, u32[]{:S(2)}, u32[]{:S(2)}) %collective-permute-start.34) | collective-permute-done | bytes 1048608 | tf_op jit(solution)/shard_map/ppermute | solution.py:398
  351.0 2.9 collective-permute-start.36
  353.9 11.3 %collective-permute-done.35 = f32[64,16,128]{2,1,0:T(8,128)S(1)} collective-permute-done((f32[64,16,128]{2,1,0:T(8,128)S(1)}, f32[64,16,128]{2,1,0:T(8,128)S(1)}, u32[]{:S(2)}, u32[]{:S(2)}) %collective-permute-start.35) | collective-permute-done | bytes 524320 | tf_op jit(solution)/shard_map/ppermute | solution.py:400
  369.6 5.8 %collective-permute-start.39 = (f32[128,16,128]{2,1,0:T(8,128)S(1)}, f32[128,16,128]{2,1,0:T(8,128)S(1)}, u32[]{:S(2)}, u32[]{:S(2)}) collective-permute-start(f32[128,16,128]{2,1,0:T(8,128)S(1)} %get-tuple-element.77), channel_id=1, source_target_pairs={{0,4},{4,8},{8,12},{12,16},{16,20},{20,24},{24,28},{32,36},{36,40}... | collective-permute-start | bytes 3145736 | tf_op jit(solution)/shard_map/ppermute | solution.py:427
  378.5 3.8 collective-permute-done.38.za_ref
  382.4 4.0 collective-permute-start.42
  386.5 5.2 collective-permute-start.41
  391.7 2.6 collective-permute-done.42.cr_ref
  395.0 10.6 %forward.7 = (f32[8320,128]{1,0:T(8,128)S(1)}, f32[16,64,128]{2,1,0:T(8,128)S(1)}, f32[16,64,128]{2,1,0:T(8,128)S(1)}) custom-call(bf16[128,480]{1,0:T(8,128)(2,1)S(1)} %get-tuple-element.135.mz_ref, bf16[64,288]{1,0:T(8,128)(2,1)S(1)} %get-tuple-element.149.mx_ref, bf16[256,256]{1,0:T(8,128)(2,1)S(1)} %get-tuple-element.133.my_ref, ...), custom_call_target="tpu_custom_call" | custom-call | flops 10000000000 | bytes 20000000 | tf_op jit(solution)/shard_map/forward/pallas_call | solution.py:305
  405.7 4.8 collective-permute-start.47
  411.8 10.6 %forward.6 = (f32[8320,128]{1,0:T(8,128)S(1)}, f32[16,64,128]{2,1,0:T(8,128)S(1)}, f32[16,64,128]{2,1,0:T(8,128)S(1)}) custom-call(bf16[128,480]{1,0:T(8,128)(2,1)S(1)} %get-tuple-element.136.mz_ref, bf16[64,288]{1,0:T(8,128)(2,1)S(1)} %get-tuple-element.150.mx_ref, bf16[256,256]{1,0:T(8,128)(2,1)S(1)} %get-tuple-element.134.my_ref, ...), custom_call_target="tpu_custom_call" | custom-call | flops 10000000000 | bytes 20000000 | tf_op jit(solution)/shard_map/forward/pallas_call | solution.py:305
  422.4 4.3 collective-permute-start.43
  428.0 3.1 back_z.7
  431.1 3.5 collective-permute-start.49
  436.6 3.1 back_z.6
  439.8 9.0 %collective-permute-start.45 = (f32[128,16,128]{2,1,0:T(8,128)S(1)}, f32[128,16,128]{2,1,0:T(8,128)S(1)}, u32[]{:S(2)}, u32[]{:S(2)}) collective-permute-start(f32[128,16,128]{2,1,0:T(8,128)S(1)} %get-tuple-element.83), channel_id=1, source_target_pairs={{0,4},{4,8},{8,12},{12,16},{16,20},{20,24},{24,28},{32,36},{36,40}... | collective-permute-start | bytes 3145736 | tf_op jit(solution)/shard_map/ppermute | solution.py:427
  450.8 6.1 %back_xy.6.rest_0_ = f32[4,128,16,128]{3,2,1,0:T(8,128)S(1)} custom-call(s32[1]{0:T(128)} %bitcast.17.me_ref, f32[8]{0:T(128)S(1)} %get-tuple-element.97.w_ref, bf16[64,288]{1,0:T(8,128)(2,1)S(1)} %get-tuple-element.151.mx_ref, bf16[256,256]{1,0:T(8,128)(2,1)S(1)} %get-tuple-element.139.my_ref, f32[8320,128]{1,0:T(8,128)S(1)} %get-tuple-element.88.r_ref, ...), custom_call_target="tpu_custom_call" | custom-call | flops 5000000000 | bytes 10000000 | tf_op jit(solution)/shard_map/back_xy/pallas_call | solution.py:342
  456.9 3.6 collective-permute-done.45.xl_ref
  460.5 4.7 collective-permute-done.46.xr_ref
  465.2 6.1 %back_xy.7 = f32[4,128,16,128]{3,2,1,0:T(8,128)S(1)} custom-call(s32[1]{0:T(128)} %bitcast.17.me_ref, f32[8]{0:T(128)S(1)} %get-tuple-element.98.w_ref, bf16[64,288]{1,0:T(8,128)(2,1)S(1)} %get-tuple-element.152.mx_ref, bf16[256,256]{1,0:T(8,128)(2,1)S(1)} %get-tuple-element.140.my_ref, f32[8320,128]{1,0:T(8,128)S(1)} %get-tuple-element.82.r_ref, ...), custom_call_target="tpu_custom_call" | custom-call | flops 5000000000 | bytes 10000000 | tf_op jit(solution)/shard_map/back_xy/pallas_call | solution.py:342
  472.4 2.6 collective-permute-start.53
  475.0 12.4 %collective-permute-done.51 = f32[64,16,128]{2,1,0:T(8,128)S(1)} collective-permute-done((f32[64,16,128]{2,1,0:T(8,128)S(1)}, f32[64,16,128]{2,1,0:T(8,128)S(1)}, u32[]{:S(2)}, u32[]{:S(2)}) %collective-permute-start.51) | collective-permute-done | bytes 524320 | tf_op jit(solution)/shard_map/ppermute | solution.py:407
  488.4 2.2 collective-permute-start.54
  490.6 12.4 %collective-permute-done.52 = f32[128,16,128]{2,1,0:T(8,128)S(1)} collective-permute-done((f32[128,16,128]{2,1,0:T(8,128)S(1)}, f32[128,16,128]{2,1,0:T(8,128)S(1)}, u32[]{:S(2)}, u32[]{:S(2)}) %collective-permute-start.52) | collective-permute-done | bytes 1048608 | tf_op jit(solution)/shard_map/ppermute | solution.py:411
  503.4 26.0 %all_to_all.33 = f32[128,16,128]{2,1,0:T(8,128)S(1)} all-to-all(f32[128,16,128]{2,1,0:T(8,128)S(1)} %fusion.4), channel_id=1, replica_groups={{0,4,8,12,16,20,24,28},{32,36,40,44,48,52,56,60},{64,68,72,76,80,84,88,..., dimensions={0} | all-to-all | bytes 2097152 | tf_op jit(solution)/shard_map/all_to_all | solution.py:523
  532.5 22.3 %collective-permute-done.56 = f32[16,128,128]{2,1,0:T(8,128)S(1)} collective-permute-done((f32[16,128,128]{2,1,0:T(8,128)S(1)}, f32[16,128,128]{2,1,0:T(8,128)S(1)}, u32[]{:S(2)}, u32[]{:S(2)}) %collective-permute-start.56) | collective-permute-done | bytes 1048608 | tf_op jit(solution)/shard_map/ppermute | solution.py:398
  554.9 2.7 collective-permute-start.58
  557.6 10.2 %collective-permute-done.57 = f32[8,128,128]{2,1,0:T(8,128)S(1)} collective-permute-done((f32[8,128,128]{2,1,0:T(8,128)S(1)}, f32[8,128,128]{2,1,0:T(8,128)S(1)}, u32[]{:S(2)}, u32[]{:S(2)}) %collective-permute-start.57) | collective-permute-done | bytes 524320 | tf_op jit(solution)/shard_map/ppermute | solution.py:400
  567.9 5.0 turn.1
  (226 shorter events, 97.4 us)
Async XLA Ops:
  8.6 27.4 %all-to-all-start = ((f32[17,128,128]{2,0,1:T(8,128)}), f32[17,128,128]{2,0,1:T(8,128)S(1)}, u32[]{:S(2)}, u32[]{:S(2)}) async-start(f32[17,128,128]{2,0,1:T(8,128)} %copy.71), calls=%async_computation | async-start | bytes 3145728 | tf_op jit(solution)/shard_map/all_to_all | solution.py:415
  37.2 25.2 %collective-permute-start.1 = (f32[128,16,128]{2,1,0:T(8,128)S(1)}, f32[128,16,128]{2,1,0:T(8,128)S(1)}, u32[]{:S(2)}, u32[]{:S(2)}) collective-permute-start(f32[128,16,128]{2,1,0:T(8,128)S(1)} %bitcast.157), channel_id=1, source_target_pairs={{0,1},{1,2},{2,3},{3,0},{4,5},{5,6},{6,7},{7,4},{8,9},{9,10},{10,1... | collective-permute-start | bytes 3145736 | tf_op jit(solution)/shard_map/ppermute | solution.py:398
  38.5 24.7 %collective-permute-start = (f32[128,16,128]{2,1,0:T(8,128)S(1)}, f32[128,16,128]{2,1,0:T(8,128)S(1)}, u32[]{:S(2)}, u32[]{:S(2)}) collective-permute-start(f32[128,16,128]{2,1,0:T(8,128)S(1)} %bitcast.158), channel_id=1, source_target_pairs={{1,0},{2,1},{3,2},{0,3},{5,4},{6,5},{7,6},{4,7},{9,8},{10,9},{11,1... | collective-permute-start | bytes 3145736 | tf_op jit(solution)/shard_map/ppermute | solution.py:399
  56.3 13.1 %collective-permute-start.10 = (f32[16,64,128]{2,1,0:T(8,128)}, f32[16,64,128]{2,1,0:T(8,128)}, u32[]{:S(2)}, u32[]{:S(2)}) collective-permute-start(f32[16,64,128]{2,1,0:T(8,128)} %get-tuple-element.117), channel_id=1, source_target_pairs={{0,4},{4,8},{8,12},{12,16},{16,20},{20,24},{24,28},{28,0},{32,36},... | collective-permute-start | bytes 1572872 | tf_op jit(solution)/shard_map/ppermute | solution.py:467
  57.9 26.4 %collective-permute-start.11 = (f32[16,64,128]{2,1,0:T(8,128)}, f32[16,64,128]{2,1,0:T(8,128)}, u32[]{:S(2)}, u32[]{:S(2)}) collective-permute-start(f32[16,64,128]{2,1,0:T(8,128)} %get-tuple-element.116), channel_id=1, source_target_pairs={{0,8},{4,12},{8,16},{12,20},{16,24},{20,28},{24,0},{28,4},{32,40},... | collective-permute-start | bytes 1572872 | tf_op jit(solution)/shard_map/ppermute | solution.py:467
  57.9 41.7 %collective-permute-start.12 = (f32[16,64,128]{2,1,0:T(8,128)}, f32[16,64,128]{2,1,0:T(8,128)}, u32[]{:S(2)}, u32[]{:S(2)}) collective-permute-start(f32[16,64,128]{2,1,0:T(8,128)} %get-tuple-element.115), channel_id=1, source_target_pairs={{0,12},{4,16},{8,20},{12,24},{16,28},{20,0},{24,4},{28,8},{32,44},... | collective-permute-start | bytes 1572872 | tf_op jit(solution)/shard_map/ppermute | solution.py:467
  63.2 40.1 %collective-permute-start.2 = (f32[64,16,128]{2,1,0:T(8,128)}, f32[64,16,128]{2,1,0:T(8,128)}, u32[]{:S(2)}, u32[]{:S(2)}) collective-permute-start(f32[64,16,128]{2,1,0:T(8,128)} %slice.219), channel_id=1, source_target_pairs={{0,1},{1,2},{2,3},{3,0},{4,5},{5,6},{6,7},{7,4},{8,9},{9,10},{10,1... | collective-permute-start | bytes 1572872 | tf_op jit(solution)/shard_map/ppermute | solution.py:400
  64.0 51.3 %collective-permute-start.3 = (f32[64,16,128]{2,1,0:T(8,128)}, f32[64,16,128]{2,1,0:T(8,128)}, u32[]{:S(2)}, u32[]{:S(2)}) collective-permute-start(f32[64,16,128]{2,1,0:T(8,128)} %slice.220), channel_id=1, source_target_pairs={{1,0},{2,1},{3,2},{0,3},{5,4},{6,5},{7,6},{4,7},{9,8},{10,9},{11,1... | collective-permute-start | bytes 1572872 | tf_op jit(solution)/shard_map/ppermute | solution.py:401
  69.3 51.2 %collective-permute-start.13 = (f32[16,64,128]{2,1,0:T(8,128)}, f32[16,64,128]{2,1,0:T(8,128)}, u32[]{:S(2)}, u32[]{:S(2)}) collective-permute-start(f32[16,64,128]{2,1,0:T(8,128)} %get-tuple-element.114), channel_id=1, source_target_pairs={{0,16},{4,20},{8,24},{12,28},{16,0},{20,4},{24,8},{28,12},{32,48},... | collective-permute-start | bytes 1572872 | tf_op jit(solution)/shard_map/ppermute | solution.py:467
  84.3 37.6 %collective-permute-start.14 = (f32[16,64,128]{2,1,0:T(8,128)}, f32[16,64,128]{2,1,0:T(8,128)}, u32[]{:S(2)}, u32[]{:S(2)}) collective-permute-start(f32[16,64,128]{2,1,0:T(8,128)} %get-tuple-element.113), channel_id=1, source_target_pairs={{0,20},{4,24},{8,28},{12,0},{16,4},{20,8},{24,12},{28,16},{32,52},... | collective-permute-start | bytes 1572872 | tf_op jit(solution)/shard_map/ppermute | solution.py:467
  99.6 44.8 %collective-permute-start.21 = (f32[128,16,128]{2,1,0:T(8,128)}, f32[128,16,128]{2,1,0:T(8,128)}, u32[]{:S(2)}, u32[]{:S(2)}) collective-permute-start(f32[128,16,128]{2,1,0:T(8,128)} %get-tuple-element.63), channel_id=1, source_target_pairs={{0,0},{4,32},{8,64},{12,96},{16,4},{20,36},{24,68},{28,100},{32,40... | collective-permute-start | bytes 3145736 | tf_op jit(solution)/shard_map/ppermute | solution.py:459
  103.3 30.8 %collective-permute-start.15 = (f32[16,64,128]{2,1,0:T(8,128)}, f32[16,64,128]{2,1,0:T(8,128)}, u32[]{:S(2)}, u32[]{:S(2)}) collective-permute-start(f32[16,64,128]{2,1,0:T(8,128)} %get-tuple-element.112), channel_id=1, source_target_pairs={{0,24},{4,28},{8,0},{12,4},{16,8},{20,12},{24,16},{28,20},{32,56},... | collective-permute-start | bytes 1572872 | tf_op jit(solution)/shard_map/ppermute | solution.py:467
  115.4 25.8 %collective-permute-start.16 = (f32[16,64,128]{2,1,0:T(8,128)}, f32[16,64,128]{2,1,0:T(8,128)}, u32[]{:S(2)}, u32[]{:S(2)}) collective-permute-start(f32[16,64,128]{2,1,0:T(8,128)} %get-tuple-element.111), channel_id=1, source_target_pairs={{0,28},{4,0},{8,4},{12,8},{16,12},{20,16},{24,20},{28,24},{32,60},... | collective-permute-start | bytes 1572872 | tf_op jit(solution)/shard_map/ppermute | solution.py:467
  116.3 28.1 %copy-start.13 = (bf16[2,128,480]{2,1,0:T(8,128)(2,1)S(1)}, bf16[2,128,480]{2,1,0:T(8,128)(2,1)}, u32[]{:S(2)}) copy-start(bf16[2,128,480]{2,1,0:T(8,128)(2,1)} %pad_maximum_fusion.9) | copy-start | bytes 737284
  116.3 28.1 %copy-start.10 = (f32[128,16,128]{2,1,0:T(8,128)S(1)}, f32[128,16,128]{2,1,0:T(8,128)}, u32[]{:S(2)}) copy-start(f32[128,16,128]{2,1,0:T(8,128)} %get-tuple-element.66) | copy-start | bytes 3145732
  118.9 81.3 %copy-start.3 = (f32[16,64,128]{2,1,0:T(8,128)S(1)}, f32[16,64,128]{2,1,0:T(8,128)}, u32[]{:S(2)}) copy-start(f32[16,64,128]{2,1,0:T(8,128)} %get-tuple-element.118.refs_0_) | copy-start | bytes 1572868
  120.5 25.9 %collective-permute-start.4 = (f32[16,64,128]{2,1,0:T(8,128)S(1)}, f32[16,64,128]{2,1,0:T(8,128)S(1)}, u32[]{:S(2)}, u32[]{:S(2)}) collective-permute-start(f32[16,64,128]{2,1,0:T(8,128)S(1)} %get-tuple-element.52), channel_id=1, source_target_pairs={{0,32},{4,36},{8,40},{12,44},{16,48},{20,52},{24,56},{28,60},{32,6... | collective-permute-start | bytes 1572872 | tf_op jit(solution)/shard_map/ppermute | solution.py:421
  121.9 28.5 %collective-permute-start.5 = (f32[16,64,128]{2,1,0:T(8,128)S(1)}, f32[16,64,128]{2,1,0:T(8,128)S(1)}, u32[]{:S(2)}, u32[]{:S(2)}) collective-permute-start(f32[16,64,128]{2,1,0:T(8,128)S(1)} %get-tuple-element.53), channel_id=1, source_target_pairs={{32,0},{36,4},{40,8},{44,12},{48,16},{52,20},{56,24},{60,28},{64,3... | collective-permute-start | bytes 1572872 | tf_op jit(solution)/shard_map/ppermute | solution.py:422
  134.1 30.0 %collective-permute-start.22 = (f32[128,16,128]{2,1,0:T(8,128)S(1)}, f32[128,16,128]{2,1,0:T(8,128)S(1)}, u32[]{:S(2)}, u32[]{:S(2)}) collective-permute-start(f32[128,16,128]{2,1,0:T(8,128)S(1)} %copy-done.12), channel_id=1, source_target_pairs={{0,32},{4,64},{8,96},{12,0},{16,36},{20,68},{24,100},{28,4},{32,72... | collective-permute-start | bytes 3145736 | tf_op jit(solution)/shard_map/ppermute | solution.py:459
  141.1 43.1 %collective-permute-start.23 = (f32[128,16,128]{2,1,0:T(8,128)S(1)}, f32[128,16,128]{2,1,0:T(8,128)S(1)}, u32[]{:S(2)}, u32[]{:S(2)}) collective-permute-start(f32[128,16,128]{2,1,0:T(8,128)S(1)} %copy-done.11), channel_id=1, source_target_pairs={{0,64},{4,96},{8,0},{12,32},{16,68},{20,100},{24,4},{28,36},{32,10... | collective-permute-start | bytes 3145736 | tf_op jit(solution)/shard_map/ppermute | solution.py:459
  144.5 58.1 %collective-permute-start.24 = (f32[128,16,128]{2,1,0:T(8,128)S(1)}, f32[128,16,128]{2,1,0:T(8,128)S(1)}, u32[]{:S(2)}, u32[]{:S(2)}) collective-permute-start(f32[128,16,128]{2,1,0:T(8,128)S(1)} %copy-done.10), channel_id=1, source_target_pairs={{0,96},{4,0},{8,32},{12,64},{16,100},{20,4},{24,36},{28,68},{32,8}... | collective-permute-start | bytes 3145736 | tf_op jit(solution)/shard_map/ppermute | solution.py:459
  146.4 61.0 %collective-permute-start.6 = (f32[128,16,128]{2,1,0:T(8,128)S(1)}, f32[128,16,128]{2,1,0:T(8,128)S(1)}, u32[]{:S(2)}, u32[]{:S(2)}) collective-permute-start(f32[128,16,128]{2,1,0:T(8,128)S(1)} %get-tuple-element.54), channel_id=1, source_target_pairs={{0,4},{4,8},{8,12},{12,16},{16,20},{20,24},{24,28},{32,36},{36,40}... | collective-permute-start | bytes 3145736 | tf_op jit(solution)/shard_map/ppermute | solution.py:427
  150.4 57.0 %collective-permute-start.7 = (f32[128,16,128]{2,1,0:T(8,128)S(1)}, f32[128,16,128]{2,1,0:T(8,128)S(1)}, u32[]{:S(2)}, u32[]{:S(2)}) collective-permute-start(f32[128,16,128]{2,1,0:T(8,128)S(1)} %get-tuple-element.55), channel_id=1, source_target_pairs={{4,0},{8,4},{12,8},{16,12},{20,16},{24,20},{28,24},{36,32},{40,36}... | collective-permute-start | bytes 3145736 | tf_op jit(solution)/shard_map/ppermute | solution.py:428
  164.1 43.2 %collective-permute-start.9 = (f32[32,16,128]{2,1,0:T(8,128)S(1)}, f32[32,16,128]{2,1,0:T(8,128)S(1)}, u32[]{:S(2)}, u32[]{:S(2)}) collective-permute-start(f32[32,16,128]{2,1,0:T(8,128)S(1)} %pad_maximum_fusion.11), channel_id=1, source_target_pairs={{4,0},{8,4},{12,8},{16,12},{20,16},{24,20},{28,24},{36,32},{40,36}... | collective-permute-start | bytes 786440 | tf_op jit(solution)/shard_map/ppermute | solution.py:428
  184.3 23.1 %collective-permute-start.8 = (f32[32,16,128]{2,1,0:T(8,128)S(1)}, f32[32,16,128]{2,1,0:T(8,128)S(1)}, u32[]{:S(2)}, u32[]{:S(2)}) collective-permute-start(f32[32,16,128]{2,1,0:T(8,128)S(1)} %pad_maximum_fusion.10), channel_id=1, source_target_pairs={{0,4},{4,8},{8,12},{12,16},{16,20},{20,24},{24,28},{32,36},{36,40}... | collective-permute-start | bytes 786440 | tf_op jit(solution)/shard_map/ppermute | solution.py:427
  218.0 18.8 %collective-permute-start.25 = (f32[16,64,128]{2,1,0:T(8,128)S(1)}, f32[16,64,128]{2,1,0:T(8,128)S(1)}, u32[]{:S(2)}, u32[]{:S(2)}) collective-permute-start(f32[16,64,128]{2,1,0:T(8,128)S(1)} %get-tuple-element.69), channel_id=1, source_target_pairs={{0,32},{4,36},{8,40},{12,44},{16,48},{20,52},{24,56},{28,60},{32,6... | collective-permute-start | bytes 1572872 | tf_op jit(solution)/shard_map/ppermute | solution.py:421
  219.4 17.4 %collective-permute-start.26 = (f32[16,64,128]{2,1,0:T(8,128)S(1)}, f32[16,64,128]{2,1,0:T(8,128)S(1)}, u32[]{:S(2)}, u32[]{:S(2)}) collective-permute-start(f32[16,64,128]{2,1,0:T(8,128)S(1)} %get-tuple-element.70), channel_id=1, source_target_pairs={{32,0},{36,4},{40,8},{44,12},{48,16},{52,20},{56,24},{60,28},{64,3... | collective-permute-start | bytes 1572872 | tf_op jit(solution)/shard_map/ppermute | solution.py:422
  231.3 17.4 %collective-permute-start.17 = (f32[16,64,128]{2,1,0:T(8,128)S(1)}, f32[16,64,128]{2,1,0:T(8,128)S(1)}, u32[]{:S(2)}, u32[]{:S(2)}) collective-permute-start(f32[16,64,128]{2,1,0:T(8,128)S(1)} %get-tuple-element.58), channel_id=1, source_target_pairs={{0,32},{4,36},{8,40},{12,44},{16,48},{20,52},{24,56},{28,60},{32,6... | collective-permute-start | bytes 1572872 | tf_op jit(solution)/shard_map/ppermute | solution.py:421
  235.3 15.0 %collective-permute-start.18 = (f32[16,64,128]{2,1,0:T(8,128)S(1)}, f32[16,64,128]{2,1,0:T(8,128)S(1)}, u32[]{:S(2)}, u32[]{:S(2)}) collective-permute-start(f32[16,64,128]{2,1,0:T(8,128)S(1)} %get-tuple-element.59), channel_id=1, source_target_pairs={{32,0},{36,4},{40,8},{44,12},{48,16},{52,20},{56,24},{60,28},{64,3... | collective-permute-start | bytes 1572872 | tf_op jit(solution)/shard_map/ppermute | solution.py:422
  243.3 20.4 %collective-permute-start.27 = (f32[128,16,128]{2,1,0:T(8,128)}, f32[128,16,128]{2,1,0:T(8,128)}, u32[]{:S(2)}, u32[]{:S(2)}) collective-permute-start(f32[128,16,128]{2,1,0:T(8,128)} %get-tuple-element.72), channel_id=1, source_target_pairs={{0,4},{4,8},{8,12},{12,16},{16,20},{20,24},{24,28},{32,36},{36,40}... | collective-permute-start | bytes 3145736 | tf_op jit(solution)/shard_map/ppermute | solution.py:427
  246.5 17.2 %collective-permute-start.28 = (f32[128,16,128]{2,1,0:T(8,128)}, f32[128,16,128]{2,1,0:T(8,128)}, u32[]{:S(2)}, u32[]{:S(2)}) collective-permute-start(f32[128,16,128]{2,1,0:T(8,128)} %get-tuple-element.73), channel_id=1, source_target_pairs={{4,0},{8,4},{12,8},{16,12},{20,16},{24,20},{28,24},{36,32},{40,36}... | collective-permute-start | bytes 3145736 | tf_op jit(solution)/shard_map/ppermute | solution.py:428
  256.9 16.1 %collective-permute-start.19 = (f32[128,16,128]{2,1,0:T(8,128)}, f32[128,16,128]{2,1,0:T(8,128)}, u32[]{:S(2)}, u32[]{:S(2)}) collective-permute-start(f32[128,16,128]{2,1,0:T(8,128)} %get-tuple-element.61), channel_id=1, source_target_pairs={{0,4},{4,8},{8,12},{12,16},{16,20},{20,24},{24,28},{32,36},{36,40}... | collective-permute-start | bytes 3145736 | tf_op jit(solution)/shard_map/ppermute | solution.py:427
  258.8 16.4 %collective-permute-start.20 = (f32[128,16,128]{2,1,0:T(8,128)}, f32[128,16,128]{2,1,0:T(8,128)}, u32[]{:S(2)}, u32[]{:S(2)}) collective-permute-start(f32[128,16,128]{2,1,0:T(8,128)} %get-tuple-element.62), channel_id=1, source_target_pairs={{4,0},{8,4},{12,8},{16,12},{20,16},{24,20},{28,24},{36,32},{40,36}... | collective-permute-start | bytes 3145736 | tf_op jit(solution)/shard_map/ppermute | solution.py:428
  282.5 12.6 %collective-permute-start.29 = (f32[64,16,128]{2,1,0:T(8,128)S(1)}, f32[64,16,128]{2,1,0:T(8,128)S(1)}, u32[]{:S(2)}, u32[]{:S(2)}) collective-permute-start(f32[64,16,128]{2,1,0:T(8,128)S(1)} %get-tuple-element.107), channel_id=1, source_target_pairs={{0,1},{1,2},{2,3},{3,0},{4,5},{5,6},{6,7},{7,4},{8,9},{9,10},{10,1... | collective-permute-start | bytes 1572872 | tf_op jit(solution)/shard_map/ppermute | solution.py:407
  282.7 12.5 %collective-permute-start.31 = (f32[64,16,128]{2,1,0:T(8,128)S(1)}, f32[64,16,128]{2,1,0:T(8,128)S(1)}, u32[]{:S(2)}, u32[]{:S(2)}) collective-permute-start(f32[64,16,128]{2,1,0:T(8,128)S(1)} %get-tuple-element.108), channel_id=1, source_target_pairs={{1,0},{2,1},{3,2},{0,3},{5,4},{6,5},{7,6},{4,7},{9,8},{10,9},{11,1... | collective-permute-start | bytes 1572872 | tf_op jit(solution)/shard_map/ppermute | solution.py:408
  295.3 25.4 %collective-permute-start.30 = (f32[128,16,128]{2,1,0:T(8,128)S(1)}, f32[128,16,128]{2,1,0:T(8,128)}, u32[]{:S(2)}, u32[]{:S(2)}) collective-permute-start(f32[128,16,128]{2,1,0:T(8,128)S(1)} %pad_maximum_fusion.2), channel_id=1, source_target_pairs={{0,1},{1,2},{2,3},{3,0},{4,5},{5,6},{6,7},{7,4},{8,9},{9,10},{10,1... | collective-permute-start | bytes 3145736 | tf_op jit(solution)/shard_map/ppermute | solution.py:411
  296.9 24.9 %collective-permute-start.32 = (f32[128,16,128]{2,1,0:T(8,128)}, f32[128,16,128]{2,1,0:T(8,128)}, u32[]{:S(2)}, u32[]{:S(2)}) collective-permute-start(f32[128,16,128]{2,1,0:T(8,128)} %pad_maximum_fusion.3), channel_id=1, source_target_pairs={{1,0},{2,1},{3,2},{0,3},{5,4},{6,5},{7,6},{4,7},{9,8},{10,9},{11,1... | collective-permute-start | bytes 3145736 | tf_op jit(solution)/shard_map/ppermute | solution.py:411
  324.0 26.8 %collective-permute-start.34 = (f32[128,16,128]{2,1,0:T(8,128)S(1)}, f32[128,16,128]{2,1,0:T(8,128)S(1)}, u32[]{:S(2)}, u32[]{:S(2)}) collective-permute-start(f32[128,16,128]{2,1,0:T(8,128)S(1)} %fusion.9.refs_0_), channel_id=1, source_target_pairs={{0,1},{1,2},{2,3},{3,0},{4,5},{5,6},{6,7},{7,4},{8,9},{9,10},{10,1... | collective-permute-start | bytes 3145736 | tf_op jit(solution)/shard_map/ppermute | solution.py:398
  325.3 25.6 %collective-permute-start.33 = (f32[128,16,128]{2,1,0:T(8,128)S(1)}, f32[128,16,128]{2,1,0:T(8,128)S(1)}, u32[]{:S(2)}, u32[]{:S(2)}) collective-permute-start(f32[128,16,128]{2,1,0:T(8,128)S(1)} %fusion.9.refs_0_), channel_id=1, source_target_pairs={{1,0},{2,1},{3,2},{0,3},{5,4},{6,5},{7,6},{4,7},{9,8},{10,9},{11,1... | collective-permute-start | bytes 3145736 | tf_op jit(solution)/shard_map/ppermute | solution.py:399
  350.9 14.4 %collective-permute-start.35 = (f32[64,16,128]{2,1,0:T(8,128)S(1)}, f32[64,16,128]{2,1,0:T(8,128)S(1)}, u32[]{:S(2)}, u32[]{:S(2)}) collective-permute-start(f32[64,16,128]{2,1,0:T(8,128)S(1)} %slice.238), channel_id=1, source_target_pairs={{0,1},{1,2},{2,3},{3,0},{4,5},{5,6},{6,7},{7,4},{8,9},{9,10},{10,1... | collective-permute-start | bytes 1572872 | tf_op jit(solution)/shard_map/ppermute | solution.py:400
  351.0 44.0 %copy-start.5 = (f32[128,64,128]{2,1,0:T(8,128)S(1)}, f32[128,64,128]{2,1,0:T(8,128)}, u32[]{:S(2)}) copy-start(f32[128,64,128]{2,1,0:T(8,128)} %copy-done.4) | copy-start | bytes 12582916
  351.0 14.2 %collective-permute-start.36 = (f32[64,16,128]{2,1,0:T(8,128)S(1)}, f32[64,16,128]{2,1,0:T(8,128)S(1)}, u32[]{:S(2)}, u32[]{:S(2)}) collective-permute-start(f32[64,16,128]{2,1,0:T(8,128)S(1)} %slice.239), channel_id=1, source_target_pairs={{1,0},{2,1},{3,2},{0,3},{5,4},{6,5},{7,6},{4,7},{9,8},{10,9},{11,1... | collective-permute-start | bytes 1572872 | tf_op jit(solution)/shard_map/ppermute | solution.py:401
  366.9 11.6 %collective-permute-start.37 = (f32[16,64,128]{2,1,0:T(8,128)S(1)}, f32[16,64,128]{2,1,0:T(8,128)S(1)}, u32[]{:S(2)}, u32[]{:S(2)}) collective-permute-start(f32[16,64,128]{2,1,0:T(8,128)S(1)} %get-tuple-element.75), channel_id=1, source_target_pairs={{0,32},{4,36},{8,40},{12,44},{16,48},{20,52},{24,56},{28,60},{32,6... | collective-permute-start | bytes 1572872 | tf_op jit(solution)/shard_map/ppermute | solution.py:421
  368.2 14.1 %collective-permute-start.38 = (f32[16,64,128]{2,1,0:T(8,128)S(1)}, f32[16,64,128]{2,1,0:T(8,128)S(1)}, u32[]{:S(2)}, u32[]{:S(2)}) collective-permute-start(f32[16,64,128]{2,1,0:T(8,128)S(1)} %get-tuple-element.76), channel_id=1, source_target_pairs={{32,0},{36,4},{40,8},{44,12},{48,16},{52,20},{56,24},{60,28},{64,3... | collective-permute-start | bytes 1572872 | tf_op jit(solution)/shard_map/ppermute | solution.py:422
  369.6 25.5 %collective-permute-start.39 = (f32[128,16,128]{2,1,0:T(8,128)S(1)}, f32[128,16,128]{2,1,0:T(8,128)S(1)}, u32[]{:S(2)}, u32[]{:S(2)}) collective-permute-start(f32[128,16,128]{2,1,0:T(8,128)S(1)} %get-tuple-element.77), channel_id=1, source_target_pairs={{0,4},{4,8},{8,12},{12,16},{16,20},{20,24},{24,28},{32,36},{36,40}... | collective-permute-start | bytes 3145736 | tf_op jit(solution)/shard_map/ppermute | solution.py:427
  375.4 19.6 %collective-permute-start.40 = (f32[128,16,128]{2,1,0:T(8,128)S(1)}, f32[128,16,128]{2,1,0:T(8,128)S(1)}, u32[]{:S(2)}, u32[]{:S(2)}) collective-permute-start(f32[128,16,128]{2,1,0:T(8,128)S(1)} %get-tuple-element.78), channel_id=1, source_target_pairs={{4,0},{8,4},{12,8},{16,12},{20,16},{24,20},{28,24},{36,32},{40,36}... | collective-permute-start | bytes 3145736 | tf_op jit(solution)/shard_map/ppermute | solution.py:428
  382.4 11.9 %collective-permute-start.42 = (f32[32,16,128]{2,1,0:T(8,128)S(1)}, f32[32,16,128]{2,1,0:T(8,128)S(1)}, u32[]{:S(2)}, u32[]{:S(2)}) collective-permute-start(f32[32,16,128]{2,1,0:T(8,128)S(1)} %pad_maximum_fusion.13), channel_id=1, source_target_pairs={{4,0},{8,4},{12,8},{16,12},{20,16},{24,20},{28,24},{36,32},{40,36}... | collective-permute-start | bytes 786440 | tf_op jit(solution)/shard_map/ppermute | solution.py:428
  386.5 8.5 %collective-permute-start.41 = (f32[32,16,128]{2,1,0:T(8,128)S(1)}, f32[32,16,128]{2,1,0:T(8,128)S(1)}, u32[]{:S(2)}, u32[]{:S(2)}) collective-permute-start(f32[32,16,128]{2,1,0:T(8,128)S(1)} %pad_maximum_fusion.12), channel_id=1, source_target_pairs={{0,4},{4,8},{8,12},{12,16},{16,20},{20,24},{24,28},{32,36},{36,40}... | collective-permute-start | bytes 786440 | tf_op jit(solution)/shard_map/ppermute | solution.py:427
  405.7 22.4 %collective-permute-start.47 = (f32[16,64,128]{2,1,0:T(8,128)S(1)}, f32[16,64,128]{2,1,0:T(8,128)S(1)}, u32[]{:S(2)}, u32[]{:S(2)}) collective-permute-start(f32[16,64,128]{2,1,0:T(8,128)S(1)} %get-tuple-element.86), channel_id=1, source_target_pairs={{0,32},{4,36},{8,40},{12,44},{16,48},{20,52},{24,56},{28,60},{32,6... | collective-permute-start | bytes 1572872 | tf_op jit(solution)/shard_map/ppermute | solution.py:421
  410.5 17.5 %collective-permute-start.48 = (f32[16,64,128]{2,1,0:T(8,128)S(1)}, f32[16,64,128]{2,1,0:T(8,128)S(1)}, u32[]{:S(2)}, u32[]{:S(2)}) collective-permute-start(f32[16,64,128]{2,1,0:T(8,128)S(1)} %get-tuple-element.87), channel_id=1, source_target_pairs={{32,0},{36,4},{40,8},{44,12},{48,16},{52,20},{56,24},{60,28},{64,3... | collective-permute-start | bytes 1572872 | tf_op jit(solution)/shard_map/ppermute | solution.py:422
  422.4 14.2 %collective-permute-start.43 = (f32[16,64,128]{2,1,0:T(8,128)S(1)}, f32[16,64,128]{2,1,0:T(8,128)S(1)}, u32[]{:S(2)}, u32[]{:S(2)}) collective-permute-start(f32[16,64,128]{2,1,0:T(8,128)S(1)} %get-tuple-element.80), channel_id=1, source_target_pairs={{0,32},{4,36},{8,40},{12,44},{16,48},{20,52},{24,56},{28,60},{32,6... | collective-permute-start | bytes 1572872 | tf_op jit(solution)/shard_map/ppermute | solution.py:421
  426.7 9.9 %collective-permute-start.44 = (f32[16,64,128]{2,1,0:T(8,128)S(1)}, f32[16,64,128]{2,1,0:T(8,128)S(1)}, u32[]{:S(2)}, u32[]{:S(2)}) collective-permute-start(f32[16,64,128]{2,1,0:T(8,128)S(1)} %get-tuple-element.81), channel_id=1, source_target_pairs={{32,0},{36,4},{40,8},{44,12},{48,16},{52,20},{56,24},{60,28},{64,3... | collective-permute-start | bytes 1572872 | tf_op jit(solution)/shard_map/ppermute | solution.py:422
  431.1 19.5 %collective-permute-start.49 = (f32[128,16,128]{2,1,0:T(8,128)S(1)}, f32[128,16,128]{2,1,0:T(8,128)S(1)}, u32[]{:S(2)}, u32[]{:S(2)}) collective-permute-start(f32[128,16,128]{2,1,0:T(8,128)S(1)} %get-tuple-element.89), channel_id=1, source_target_pairs={{0,4},{4,8},{8,12},{12,16},{16,20},{20,24},{24,28},{32,36},{36,40}... | collective-permute-start | bytes 3145736 | tf_op jit(solution)/shard_map/ppermute | solution.py:427
  434.7 16.1 %collective-permute-start.50 = (f32[128,16,128]{2,1,0:T(8,128)S(1)}, f32[128,16,128]{2,1,0:T(8,128)S(1)}, u32[]{:S(2)}, u32[]{:S(2)}) collective-permute-start(f32[128,16,128]{2,1,0:T(8,128)S(1)} %get-tuple-element.90), channel_id=1, source_target_pairs={{4,0},{8,4},{12,8},{16,12},{20,16},{24,20},{28,24},{36,32},{40,36}... | collective-permute-start | bytes 3145736 | tf_op jit(solution)/shard_map/ppermute | solution.py:428
  439.8 20.7 %collective-permute-start.45 = (f32[128,16,128]{2,1,0:T(8,128)S(1)}, f32[128,16,128]{2,1,0:T(8,128)S(1)}, u32[]{:S(2)}, u32[]{:S(2)}) collective-permute-start(f32[128,16,128]{2,1,0:T(8,128)S(1)} %get-tuple-element.83), channel_id=1, source_target_pairs={{0,4},{4,8},{8,12},{12,16},{16,20},{20,24},{24,28},{32,36},{36,40}... | collective-permute-start | bytes 3145736 | tf_op jit(solution)/shard_map/ppermute | solution.py:427
  448.8 16.4 %collective-permute-start.46 = (f32[128,16,128]{2,1,0:T(8,128)S(1)}, f32[128,16,128]{2,1,0:T(8,128)S(1)}, u32[]{:S(2)}, u32[]{:S(2)}) collective-permute-start(f32[128,16,128]{2,1,0:T(8,128)S(1)} %get-tuple-element.84), channel_id=1, source_target_pairs={{4,0},{8,4},{12,8},{16,12},{20,16},{24,20},{28,24},{36,32},{40,36}... | collective-permute-start | bytes 3145736 | tf_op jit(solution)/shard_map/ppermute | solution.py:428
  471.4 16.0 %collective-permute-start.51 = (f32[64,16,128]{2,1,0:T(8,128)S(1)}, f32[64,16,128]{2,1,0:T(8,128)S(1)}, u32[]{:S(2)}, u32[]{:S(2)}) collective-permute-start(f32[64,16,128]{2,1,0:T(8,128)S(1)} %get-tuple-element.101), channel_id=1, source_target_pairs={{0,1},{1,2},{2,3},{3,0},{4,5},{5,6},{6,7},{7,4},{8,9},{9,10},{10,1... | collective-permute-start | bytes 1572872 | tf_op jit(solution)/shard_map/ppermute | solution.py:407
  472.4 15.0 %collective-permute-start.53 = (f32[64,16,128]{2,1,0:T(8,128)S(1)}, f32[64,16,128]{2,1,0:T(8,128)S(1)}, u32[]{:S(2)}, u32[]{:S(2)}) collective-permute-start(f32[64,16,128]{2,1,0:T(8,128)S(1)} %get-tuple-element.102), channel_id=1, source_target_pairs={{1,0},{2,1},{3,2},{0,3},{5,4},{6,5},{7,6},{4,7},{9,8},{10,9},{11,1... | collective-permute-start | bytes 1572872 | tf_op jit(solution)/shard_map/ppermute | solution.py:408
  487.6 15.4 %collective-permute-start.52 = (f32[128,16,128]{2,1,0:T(8,128)S(1)}, f32[128,16,128]{2,1,0:T(8,128)S(1)}, u32[]{:S(2)}, u32[]{:S(2)}) collective-permute-start(f32[128,16,128]{2,1,0:T(8,128)S(1)} %pad_maximum_fusion.5), channel_id=1, source_target_pairs={{0,1},{1,2},{2,3},{3,0},{4,5},{5,6},{6,7},{7,4},{8,9},{9,10},{10,1... | collective-permute-start | bytes 3145736 | tf_op jit(solution)/shard_map/ppermute | solution.py:411
  488.4 14.7 %collective-permute-start.54 = (f32[128,16,128]{2,1,0:T(8,128)S(1)}, f32[128,16,128]{2,1,0:T(8,128)S(1)}, u32[]{:S(2)}, u32[]{:S(2)}) collective-permute-start(f32[128,16,128]{2,1,0:T(8,128)S(1)} %pad_maximum_fusion.6), channel_id=1, source_target_pairs={{1,0},{2,1},{3,2},{0,3},{5,4},{6,5},{7,6},{4,7},{9,8},{10,9},{11,1... | collective-permute-start | bytes 3145736 | tf_op jit(solution)/shard_map/ppermute | solution.py:411
  529.5 25.2 %collective-permute-start.56 = (f32[16,128,128]{2,1,0:T(8,128)S(1)}, f32[16,128,128]{2,1,0:T(8,128)S(1)}, u32[]{:S(2)}, u32[]{:S(2)}) collective-permute-start(f32[16,128,128]{2,1,0:T(8,128)S(1)} %bitcast.160), channel_id=1, source_target_pairs={{0,1},{1,2},{2,3},{3,0},{4,5},{5,6},{6,7},{7,4},{8,9},{9,10},{10,1... | collective-permute-start | bytes 3145736 | tf_op jit(solution)/shard_map/ppermute | solution.py:398
  530.4 24.5 %collective-permute-start.55 = (f32[16,128,128]{2,1,0:T(8,128)S(1)}, f32[16,128,128]{2,1,0:T(8,128)S(1)}, u32[]{:S(2)}, u32[]{:S(2)}) collective-permute-start(f32[16,128,128]{2,1,0:T(8,128)S(1)} %bitcast.161), channel_id=1, source_target_pairs={{1,0},{2,1},{3,2},{0,3},{5,4},{6,5},{7,6},{4,7},{9,8},{10,9},{11,1... | collective-permute-start | bytes 3145736 | tf_op jit(solution)/shard_map/ppermute | solution.py:399
  554.8 13.0 %collective-permute-start.57 = (f32[8,128,128]{2,1,0:T(8,128)S(1)}, f32[8,128,128]{2,1,0:T(8,128)S(1)}, u32[]{:S(2)}, u32[]{:S(2)}) collective-permute-start(f32[8,128,128]{2,1,0:T(8,128)S(1)} %slice.251), channel_id=1, source_target_pairs={{0,1},{1,2},{2,3},{3,0},{4,5},{5,6},{6,7},{7,4},{8,9},{9,10},{10,1... | collective-permute-start | bytes 1572872 | tf_op jit(solution)/shard_map/ppermute | solution.py:400
  554.9 12.9 %collective-permute-start.58 = (f32[8,128,128]{2,1,0:T(8,128)S(1)}, f32[8,128,128]{2,1,0:T(8,128)S(1)}, u32[]{:S(2)}, u32[]{:S(2)}) collective-permute-start(f32[8,128,128]{2,1,0:T(8,128)S(1)} %slice.252), channel_id=1, source_target_pairs={{1,0},{2,1},{3,2},{0,3},{5,4},{6,5},{7,6},{4,7},{9,8},{10,9},{11,1... | collective-permute-start | bytes 1572872 | tf_op jit(solution)/shard_map/ppermute | solution.py:401
  (22 other events, 239.0 us)
where the time goes:
time: 578 us; the launch traced here: 573 us
  waiting for transfers between devices  217 us (38%)
  starting transfers between devices  162 us (28%)
  Pallas kernels  99.3 us (17%)
  local copies, waits for them, and re-layouts  43 us (7%)
  blocking collectives  26 us (4%)
  other arithmetic  24.4 us (4%)
    ppermute x8, starting transfers between devices, x_rims(): left = lax.ppermute(last, 'owner', X_UP)  48.5 us
    ppermute x3, waiting for transfers between devices, gather_quarters(): below = lax.ppermute(quarter, 'view', V_UP)  47.5 us
    pallas_call x4, Pallas kernels, forward(): pl.pallas_call(forward_kernel, in_specs=[VMEM] * 11, out_specs=[VMEM] * 3...  42.5 us
    ppermute x7, waiting for transfers between devices, local(): lax.ppermute(piece, 'owner', axial_round(d))  38.5 us
    ppermute x2, waiting for transfers between devices, scatter_quarters(): lax.ppermute(up, 'view', V_UP)  33.6 us
    ppermute x4, waiting for transfers between devices, local(): lax.ppermute(piece, 'owner', lateral_round(t))  29.9 us
    pallas_call x4, Pallas kernels, back_xy(): pl.pallas_call(back_xy_kernel, in_specs=[SMEM, SMEM] + [VMEM] * (len(args...  26.4 us
    all_to_all x1, blocking collectives, local(): lax.all_to_all(quarter, 'owner', split_axis=0, concat_axis=1, axis_index_...  26 us
  transfers between devices with their start and end apart: 60, of which 25 were waited for; matrix products, arithmetic and copies ran while one was open for 8% of the time, Pallas kernels for 10%

commit v1 on v0

--- a/solution.py
+++ b/solution.py
@@ -467,7 +467,6 @@
         lax.ppermute(piece, "owner", axial_round(d)) if d else piece
         for d, piece in enumerate(slabs)
     ]
-    axial = stack((k - jnp.arange(8)) % 8 * slab, slabs)
     lateral = assemble(jnp.stack(places), pieces)[0]
 
     count = jnp.sum(cover, axis=-1)
@@ -493,7 +492,7 @@
     )
     me_arr = me[None].astype(jnp.int32)
 
-    for _ in range(ITERS):
+    for iteration in range(ITERS):
         pieces = gather_quarters(quarter, depth // 2)
         places = ((me + jnp.arange(4)) % 4) * (width // 4)
         block, first, last, low, high = assemble(places, pieces)
@@ -504,9 +503,14 @@
             jnp.concatenate([before[:, -RIM:], after[:, -RIM:]], axis=0),
         )
         logs = None
-        for number, (obs, weight) in [*enumerate(
-            ((axial, weight_axial), (lateral, weight_lateral))
-        )][::-1]:
+        for number, weight in ((1, weight_lateral), (0, weight_axial)):
+            if number:
+                obs = lateral
+            elif iteration:
+                obs = axial
+            else:
+                slabs, _ = lax.optimization_barrier((slabs, quotient))
+                obs = axial = stack((k - jnp.arange(8)) % 8 * slab, slabs)
             quotient, first, last = forward(
                 ahead_z[number], ahead_x[number], ahead_y[number],
                 block, before, after, left, right, corner_left, corner_right, obs,

time: 578 us -> 575 us (level)
    ppermute x2, waiting for transfers between devices: 1.1 us -> 32.1 us  [scatter_quarters(): lax.ppermute(down, 'view', V_DOWN)]
    ppermute x2, waiting for transfers between devices: 33.6 us -> 6.4 us  [scatter_quarters(): lax.ppermute(up, 'view', V_UP)]
    ppermute x4, waiting for transfers between devices: 29.9 us -> 3.49 us  [local(): lax.ppermute(piece, 'owner', lateral_round(t))]
    ppermute x6, waiting for transfers between devices: 1.2 us -> 19.5 us  [z_rims(): before = lax.ppermute(last, 'owner', Z_UP)]
    ppermute x7, waiting for transfers between devices: 38.5 us -> 20.5 us  [local(): lax.ppermute(piece, 'owner', axial_round(d))]
    ppermute x8, waiting for transfers between devices: 4.32 us -> 15.1 us  [x_rims(): left = lax.ppermute(last, 'owner', X_UP)]
    unnamed x53 -> x59, local copies, waits for them, and re-layouts: 12.5 us -> 12.5 us
  transfers between devices with their start and end apart: 60 -> 60, of which waited for: 25 -> 30; matrix products, arithmetic and copies ran while one was open for 8% -> 8% of each run, Pallas kernels for 10% -> 12%
where the time goes in v1:
time: 575 us; the launch traced here: 570 us
  waiting for transfers between devices  215 us (37%)
  starting transfers between devices  167 us (29%)
  Pallas kernels  97.6 us (17%)
  local copies, waits for them, and re-layouts  41.6 us (7%)
  other arithmetic  23.7 us (4%)
  blocking collectives  23.3 us (4%)
    ppermute x8, starting transfers between devices, x_rims(): left = lax.ppermute(last, 'owner', X_UP)  53.9 us
    ppermute x3, waiting for transfers between devices, gather_quarters(): below = lax.ppermute(quarter, 'view', V_UP)  51.2 us
    pallas_call x4, Pallas kernels, forward(): pl.pallas_call(forward_kernel, in_specs=[VMEM] * 11, out_specs=[VMEM] * 3...  42.6 us
    ppermute x2, waiting for transfers between devices, scatter_quarters(): lax.ppermute(down, 'view', V_DOWN)  32.1 us
    pallas_call x4, Pallas kernels, back_xy(): pl.pallas_call(back_xy_kernel, in_specs=[SMEM, SMEM] + [VMEM] * (len(args...  26.4 us
    all_to_all x1, blocking collectives, local(): lax.all_to_all(quarter, 'owner', split_axis=0, concat_axis=1, axis_index_...  23.3 us
    ppermute x3, waiting for transfers between devices, gather_quarters(): first = lax.ppermute(below[:half], 'view', V_UP)  21.4 us
    ppermute x6, starting transfers between devices, z_rims(): before = lax.ppermute(last, 'owner', Z_UP)  20.6 us
  transfers between devices with their start and end apart: 60, of which 30 were waited for; matrix products, arithmetic and copies ran while one was open for 8% of the time, Pallas kernels for 12%

profile of v1, /device:TPU:1, one launch (start us, length us, event | category | flops | bytes accessed | tf_op | source)
XLA Modules:
  0.0 569.9 jit_solution(2092364059453788449)
XLA Ops:
  0.7 5.3 copy.69
  9.3 6.8 %all-to-all-start = ((f32[17,128,128]{2,0,1:T(8,128)}), f32[17,128,128]{2,0,1:T(8,128)S(1)}, u32[]{:S(2)}, u32[]{:S(2)}) async-start(f32[17,128,128]{2,0,1:T(8,128)} %copy.71), calls=%async_computation | async-start | bytes 3145728 | tf_op jit(solution)/shard_map/all_to_all | solution.py:415
  19.9 5.4 copy.90
  26.3 4.3 dynamic-slice_bitcast_fusion
  32.8 3.9 all-to-all-done
  50.6 4.5 collective-permute-start.17
  55.9 7.0 %collective-permute-done.1.refs_3_ = f32[128,16,128]{2,1,0:T(8,128)S(1)} collective-permute-done((f32[128,16,128]{2,1,0:T(8,128)S(1)}, f32[128,16,128]{2,1,0:T(8,128)S(1)}, u32[]{:S(2)}, u32[]{:S(2)}) %collective-permute-start.1) | collective-permute-done | bytes 1048608 | tf_op jit(solution)/shard_map/ppermute | solution.py:398
  68.0 5.3 copy.88
  73.4 4.3 dynamic-slice_bitcast_fusion.4
  81.3 4.7 collective-permute-start.18
  92.6 5.1 collective-permute-start.19
  97.7 3.1 collective-permute-start.20
  100.8 19.5 %collective-permute-done.4.zb_ref = f32[16,64,128]{2,1,0:T(8,128)S(1)} collective-permute-done((f32[16,64,128]{2,1,0:T(8,128)S(1)}, f32[16,64,128]{2,1,0:T(8,128)S(1)}, u32[]{:S(2)}, u32[]{:S(2)}) %collective-permute-start.4) | collective-permute-done | bytes 524320 | tf_op jit(solution)/shard_map/ppermute | solution.py:421
  124.9 3.5 collective-permute-done.19.refs_2_
  128.4 22.3 %collective-permute-start.8 = (f32[32,16,128]{2,1,0:T(8,128)S(1)}, f32[32,16,128]{2,1,0:T(8,128)S(1)}, u32[]{:S(2)}, u32[]{:S(2)}) collective-permute-start(f32[32,16,128]{2,1,0:T(8,128)S(1)} %pad_maximum_fusion.10), channel_id=1, source_target_pairs={{0,4},{4,8},{8,12},{12,16},{16,20},{20,24},{24,28},{32,36},{36,40}... | collective-permute-start | bytes 786440 | tf_op jit(solution)/shard_map/ppermute | solution.py:427
  152.8 4.0 assemble.4
  156.8 6.8 %collective-permute-start.14 = (f32[16,64,128]{2,1,0:T(8,128)S(1)}, f32[16,64,128]{2,1,0:T(8,128)S(1)}, u32[]{:S(2)}, u32[]{:S(2)}) collective-permute-start(f32[16,64,128]{2,1,0:T(8,128)S(1)} %copy-done.18), channel_id=1, source_target_pairs={{0,20},{4,24},{8,28},{12,0},{16,4},{20,8},{24,12},{28,16},{32,52},... | collective-permute-start | bytes 1572872 | tf_op jit(solution)/shard_map/ppermute | solution.py:467
  163.6 11.2 %collective-permute-done.8.cl_ref = f32[32,16,128]{2,1,0:T(8,128)S(1)} collective-permute-done((f32[32,16,128]{2,1,0:T(8,128)S(1)}, f32[32,16,128]{2,1,0:T(8,128)S(1)}, u32[]{:S(2)}, u32[]{:S(2)}) %collective-permute-start.8) | collective-permute-done | bytes 262176 | tf_op jit(solution)/shard_map/ppermute | solution.py:427
  175.5 5.1 collective-permute-start.11
  180.6 10.7 %forward.4 = (f32[8320,128]{1,0:T(8,128)S(1)}, f32[16,64,128]{2,1,0:T(8,128)S(1)}, f32[16,64,128]{2,1,0:T(8,128)S(1)}) custom-call(bf16[128,480]{1,0:T(8,128)(2,1)S(1)} %get-tuple-element.155.mz_ref, bf16[64,288]{1,0:T(8,128)(2,1)S(1)} %get-tuple-element.167.mx_ref, bf16[256,256]{1,0:T(8,128)(2,1)S(1)} %get-tuple-element.153.my_ref, ...), custom_call_target="tpu_custom_call" | custom-call | flops 10000000000 | bytes 20000000 | tf_op jit(solution)/shard_map/forward/pallas_call | solution.py:305
  192.2 10.5 %collective-permute-done.12.refs_3_ = f32[16,64,128]{2,1,0:T(8,128)S(1)} collective-permute-done((f32[16,64,128]{2,1,0:T(8,128)S(1)}, f32[16,64,128]{2,1,0:T(8,128)S(1)}, u32[]{:S(2)}, u32[]{:S(2)}) %collective-permute-start.12) | collective-permute-done | bytes 524320 | tf_op jit(solution)/shard_map/ppermute | solution.py:467
  202.8 3.4 collective-permute-done.11.refs_2_
  206.2 5.6 collective-permute-done.10.refs_1_
  215.8 10.7 %forward.5 = (f32[8320,128]{1,0:T(8,128)S(1)}, f32[16,64,128]{2,1,0:T(8,128)S(1)}, f32[16,64,128]{2,1,0:T(8,128)S(1)}) custom-call(bf16[128,480]{1,0:T(8,128)(2,1)S(1)} %get-tuple-element.156.mz_ref, bf16[64,288]{1,0:T(8,128)(2,1)S(1)} %get-tuple-element.168.mx_ref, bf16[256,256]{1,0:T(8,128)(2,1)S(1)} %get-tuple-element.154.my_ref, ...), custom_call_target="tpu_custom_call" | custom-call | flops 10000000000 | bytes 20000000 | tf_op jit(solution)/shard_map/forward/pallas_call | solution.py:305
  226.5 4.0 collective-permute-start.21
  232.0 4.5 back_z.5
  238.5 4.9 collective-permute-start.27
  246.0 4.5 back_z.4
  252.5 3.8 collective-permute-start.23
  262.1 7.1 %back_xy.4.rest_0_ = f32[4,128,16,128]{3,2,1,0:T(8,128)S(1)} custom-call(s32[1]{0:T(128)} %bitcast.17.me_ref, f32[8]{0:T(128)S(1)} %get-tuple-element.113.w_ref, bf16[64,288]{1,0:T(8,128)(2,1)S(1)} %get-tuple-element.165.mx_ref, bf16[256,256]{1,0:T(8,128)(2,1)S(1)} %get-tuple-element.151.my_ref, f32[8320,128]{1,0:T(8,128)S(1)} %copy-done.8, ...), custom_call_target="tpu_custom_call" | custom-call | flops 5000000000 | bytes 10000000 | tf_op jit(solution)/shard_map/back_xy/pallas_call | solution.py:342
  269.3 3.5 collective-permute-done.24.xr_ref
  272.7 7.1 %back_xy.5 = f32[4,128,16,128]{3,2,1,0:T(8,128)S(1)} custom-call(s32[1]{0:T(128)} %bitcast.17.me_ref, f32[8]{0:T(128)S(1)} %get-tuple-element.114.w_ref, bf16[64,288]{1,0:T(8,128)(2,1)S(1)} %get-tuple-element.166.mx_ref, bf16[256,256]{1,0:T(8,128)(2,1)S(1)} %get-tuple-element.152.my_ref, f32[8320,128]{1,0:T(8,128)S(1)} %bitcast.167, ...), custom_call_target="tpu_custom_call" | custom-call | flops 5000000000 | bytes 10000000 | tf_op jit(solution)/shard_map/back_xy/pallas_call | solution.py:342
  282.8 7.9 %collective-permute-done.29 = f32[64,16,128]{2,1,0:T(8,128)S(1)} collective-permute-done((f32[64,16,128]{2,1,0:T(8,128)S(1)}, f32[64,16,128]{2,1,0:T(8,128)S(1)}, u32[]{:S(2)}, u32[]{:S(2)}) %collective-permute-start.29) | collective-permute-done | bytes 524320 | tf_op jit(solution)/shard_map/ppermute | solution.py:407
  290.9 3.0 collective-permute-start.32
  295.1 18.9 %collective-permute-done.32 = f32[128,16,128]{2,1,0:T(8,128)} collective-permute-done((f32[128,16,128]{2,1,0:T(8,128)S(1)}, f32[128,16,128]{2,1,0:T(8,128)}, u32[]{:S(2)}, u32[]{:S(2)}) %collective-permute-start.32) | collective-permute-done | bytes 1048608 | tf_op jit(solution)/shard_map/ppermute | solution.py:411
  314.0 4.7 collective-permute-done.30
  323.6 22.0 %collective-permute-done.34.refs_3_ = f32[128,16,128]{2,1,0:T(8,128)S(1)} collective-permute-done((f32[128,16,128]{2,1,0:T(8,128)S(1)}, f32[128,16,128]{2,1,0:T(8,128)S(1)}, u32[]{:S(2)}, u32[]{:S(2)}) %collective-permute-start.34) | collective-permute-done | bytes 1048608 | tf_op jit(solution)/shard_map/ppermute | solution.py:398
  345.8 3.1 collective-permute-start.36
  348.9 11.4 %collective-permute-done.35 = f32[64,16,128]{2,1,0:T(8,128)S(1)} collective-permute-done((f32[64,16,128]{2,1,0:T(8,128)S(1)}, f32[64,16,128]{2,1,0:T(8,128)S(1)}, u32[]{:S(2)}, u32[]{:S(2)}) %collective-permute-start.35) | collective-permute-done | bytes 524320 | tf_op jit(solution)/shard_map/ppermute | solution.py:400
  362.3 5.5 collective-permute-start.37
  369.1 7.4 %collective-permute-start.39 = (f32[128,16,128]{2,1,0:T(8,128)S(1)}, f32[128,16,128]{2,1,0:T(8,128)S(1)}, u32[]{:S(2)}, u32[]{:S(2)}) collective-permute-start(f32[128,16,128]{2,1,0:T(8,128)S(1)} %get-tuple-element.93), channel_id=1, source_target_pairs={{0,4},{4,8},{8,12},{12,16},{16,20},{20,24},{24,28},{32,36},{36,40}... | collective-permute-start | bytes 3145736 | tf_op jit(solution)/shard_map/ppermute | solution.py:427
  378.5 4.2 collective-permute-done.38.za_ref
  382.7 6.7 %collective-permute-start.41 = (f32[32,16,128]{2,1,0:T(8,128)S(1)}, f32[32,16,128]{2,1,0:T(8,128)S(1)}, u32[]{:S(2)}, u32[]{:S(2)}) collective-permute-start(f32[32,16,128]{2,1,0:T(8,128)S(1)} %pad_maximum_fusion.12), channel_id=1, source_target_pairs={{0,4},{4,8},{8,12},{12,16},{16,20},{20,24},{24,28},{32,36},{36,40}... | collective-permute-start | bytes 786440 | tf_op jit(solution)/shard_map/ppermute | solution.py:427
  392.7 4.4 collective-permute-done.42.cr_ref
  397.2 10.6 %forward.7 = (f32[8320,128]{1,0:T(8,128)S(1)}, f32[16,64,128]{2,1,0:T(8,128)S(1)}, f32[16,64,128]{2,1,0:T(8,128)S(1)}) custom-call(bf16[128,480]{1,0:T(8,128)(2,1)S(1)} %get-tuple-element.155.mz_ref, bf16[64,288]{1,0:T(8,128)(2,1)S(1)} %get-tuple-element.167.mx_ref, bf16[256,256]{1,0:T(8,128)(2,1)S(1)} %get-tuple-element.153.my_ref, ...), custom_call_target="tpu_custom_call" | custom-call | flops 10000000000 | bytes 20000000 | tf_op jit(solution)/shard_map/forward/pallas_call | solution.py:305
  407.8 3.4 collective-permute-start.47
  412.5 10.6 %forward.6 = (f32[8320,128]{1,0:T(8,128)S(1)}, f32[16,64,128]{2,1,0:T(8,128)S(1)}, f32[16,64,128]{2,1,0:T(8,128)S(1)}) custom-call(bf16[128,480]{1,0:T(8,128)(2,1)S(1)} %get-tuple-element.156.mz_ref, bf16[64,288]{1,0:T(8,128)(2,1)S(1)} %get-tuple-element.168.mx_ref, bf16[256,256]{1,0:T(8,128)(2,1)S(1)} %get-tuple-element.154.my_ref, ...), custom_call_target="tpu_custom_call" | custom-call | flops 10000000000 | bytes 20000000 | tf_op jit(solution)/shard_map/forward/pallas_call | solution.py:305
  423.1 4.0 collective-permute-start.43
  428.5 3.1 back_z.7
  436.1 3.6 collective-permute-done.44.za_ref
  439.8 3.1 back_z.6
  442.9 4.3 collective-permute-start.45
  450.3 6.1 %back_xy.6.rest_0_ = f32[4,128,16,128]{3,2,1,0:T(8,128)S(1)} custom-call(s32[1]{0:T(128)} %bitcast.17.me_ref, f32[8]{0:T(128)S(1)} %get-tuple-element.113.w_ref, bf16[64,288]{1,0:T(8,128)(2,1)S(1)} %get-tuple-element.165.mx_ref, bf16[256,256]{1,0:T(8,128)(2,1)S(1)} %get-tuple-element.151.my_ref, f32[8320,128]{1,0:T(8,128)S(1)} %get-tuple-element.104.r_ref, ...), custom_call_target="tpu_custom_call" | custom-call | flops 5000000000 | bytes 10000000 | tf_op jit(solution)/shard_map/back_xy/pallas_call | solution.py:342
  458.9 4.7 collective-permute-done.46.xr_ref
  463.6 6.1 %back_xy.7 = f32[4,128,16,128]{3,2,1,0:T(8,128)S(1)} custom-call(s32[1]{0:T(128)} %bitcast.17.me_ref, f32[8]{0:T(128)S(1)} %get-tuple-element.114.w_ref, bf16[64,288]{1,0:T(8,128)(2,1)S(1)} %get-tuple-element.166.mx_ref, bf16[256,256]{1,0:T(8,128)(2,1)S(1)} %get-tuple-element.152.my_ref, f32[8320,128]{1,0:T(8,128)S(1)} %get-tuple-element.98.r_ref, ...), custom_call_target="tpu_custom_call" | custom-call | flops 5000000000 | bytes 10000000 | tf_op jit(solution)/shard_map/back_xy/pallas_call | solution.py:342
  469.9 3.1 collective-permute-start.53
  473.0 9.0 %collective-permute-done.51 = f32[64,16,128]{2,1,0:T(8,128)S(1)} collective-permute-done((f32[64,16,128]{2,1,0:T(8,128)S(1)}, f32[64,16,128]{2,1,0:T(8,128)S(1)}, u32[]{:S(2)}, u32[]{:S(2)}) %collective-permute-start.51) | collective-permute-done | bytes 524320 | tf_op jit(solution)/shard_map/ppermute | solution.py:407
  484.8 3.5 collective-permute-start.54
  488.4 13.2 %collective-permute-done.54 = f32[128,16,128]{2,1,0:T(8,128)S(1)} collective-permute-done((f32[128,16,128]{2,1,0:T(8,128)S(1)}, f32[128,16,128]{2,1,0:T(8,128)S(1)}, u32[]{:S(2)}, u32[]{:S(2)}) %collective-permute-start.54) | collective-permute-done | bytes 1048608 | tf_op jit(solution)/shard_map/ppermute | solution.py:411
  503.6 23.3 %all_to_all.33 = f32[128,16,128]{2,1,0:T(8,128)S(1)} all-to-all(f32[128,16,128]{2,1,0:T(8,128)S(1)} %fusion.4), channel_id=1, replica_groups={{0,4,8,12,16,20,24,28},{32,36,40,44,48,52,56,60},{64,68,72,76,80,84,88,..., dimensions={0} | all-to-all | bytes 2097152 | tf_op jit(solution)/shard_map/all_to_all | solution.py:527
  529.7 22.2 %collective-permute-done.56 = f32[16,128,128]{2,1,0:T(8,128)S(1)} collective-permute-done((f32[16,128,128]{2,1,0:T(8,128)S(1)}, f32[16,128,128]{2,1,0:T(8,128)S(1)}, u32[]{:S(2)}, u32[]{:S(2)}) %collective-permute-start.56) | collective-permute-done | bytes 1048608 | tf_op jit(solution)/shard_map/ppermute | solution.py:398
  552.1 2.7 collective-permute-start.58
  554.8 10.0 %collective-permute-done.57 = f32[8,128,128]{2,1,0:T(8,128)S(1)} collective-permute-done((f32[8,128,128]{2,1,0:T(8,128)S(1)}, f32[8,128,128]{2,1,0:T(8,128)S(1)}, u32[]{:S(2)}, u32[]{:S(2)}) %collective-permute-start.57) | collective-permute-done | bytes 524320 | tf_op jit(solution)/shard_map/ppermute | solution.py:400
  564.9 5.0 turn.1
  (232 shorter events, 105.5 us)
Async XLA Ops:
  9.3 27.4 %all-to-all-start = ((f32[17,128,128]{2,0,1:T(8,128)}), f32[17,128,128]{2,0,1:T(8,128)S(1)}, u32[]{:S(2)}, u32[]{:S(2)}) async-start(f32[17,128,128]{2,0,1:T(8,128)} %copy.71), calls=%async_computation | async-start | bytes 3145728 | tf_op jit(solution)/shard_map/all_to_all | solution.py:415
  37.9 25.1 %collective-permute-start.1 = (f32[128,16,128]{2,1,0:T(8,128)S(1)}, f32[128,16,128]{2,1,0:T(8,128)S(1)}, u32[]{:S(2)}, u32[]{:S(2)}) collective-permute-start(f32[128,16,128]{2,1,0:T(8,128)S(1)} %bitcast.157), channel_id=1, source_target_pairs={{0,1},{1,2},{2,3},{3,0},{4,5},{5,6},{6,7},{7,4},{8,9},{9,10},{10,1... | collective-permute-start | bytes 3145736 | tf_op jit(solution)/shard_map/ppermute | solution.py:398
  39.2 24.6 %collective-permute-start = (f32[128,16,128]{2,1,0:T(8,128)S(1)}, f32[128,16,128]{2,1,0:T(8,128)S(1)}, u32[]{:S(2)}, u32[]{:S(2)}) collective-permute-start(f32[128,16,128]{2,1,0:T(8,128)S(1)} %bitcast.158), channel_id=1, source_target_pairs={{1,0},{2,1},{3,2},{0,3},{5,4},{6,5},{7,6},{4,7},{9,8},{10,9},{11,1... | collective-permute-start | bytes 3145736 | tf_op jit(solution)/shard_map/ppermute | solution.py:399
  50.6 47.1 %collective-permute-start.17 = (f32[128,16,128]{2,1,0:T(8,128)}, f32[128,16,128]{2,1,0:T(8,128)}, u32[]{:S(2)}, u32[]{:S(2)}) collective-permute-start(f32[128,16,128]{2,1,0:T(8,128)} %get-tuple-element.65), channel_id=1, source_target_pairs={{0,0},{4,32},{8,64},{12,96},{16,4},{20,36},{24,68},{28,100},{32,40... | collective-permute-start | bytes 3145736 | tf_op jit(solution)/shard_map/ppermute | solution.py:459
  63.8 22.1 %collective-permute-start.2 = (f32[64,16,128]{2,1,0:T(8,128)}, f32[64,16,128]{2,1,0:T(8,128)}, u32[]{:S(2)}, u32[]{:S(2)}) collective-permute-start(f32[64,16,128]{2,1,0:T(8,128)} %slice.219), channel_id=1, source_target_pairs={{0,1},{1,2},{2,3},{3,0},{4,5},{5,6},{6,7},{7,4},{8,9},{9,10},{10,1... | collective-permute-start | bytes 1572872 | tf_op jit(solution)/shard_map/ppermute | solution.py:400
  64.6 21.3 %collective-permute-start.3 = (f32[64,16,128]{2,1,0:T(8,128)}, f32[64,16,128]{2,1,0:T(8,128)}, u32[]{:S(2)}, u32[]{:S(2)}) collective-permute-start(f32[64,16,128]{2,1,0:T(8,128)} %slice.220), channel_id=1, source_target_pairs={{1,0},{2,1},{3,2},{0,3},{5,4},{6,5},{7,6},{4,7},{9,8},{10,9},{11,1... | collective-permute-start | bytes 1572872 | tf_op jit(solution)/shard_map/ppermute | solution.py:401
  77.6 15.0 %collective-permute-start.16 = (f32[16,64,128]{2,1,0:T(8,128)}, f32[16,64,128]{2,1,0:T(8,128)}, u32[]{:S(2)}, u32[]{:S(2)}) collective-permute-start(f32[16,64,128]{2,1,0:T(8,128)} %get-tuple-element.127), channel_id=1, source_target_pairs={{0,28},{4,0},{8,4},{12,8},{16,12},{20,16},{24,20},{28,24},{32,60},... | collective-permute-start | bytes 1572872 | tf_op jit(solution)/shard_map/ppermute | solution.py:467
  81.3 43.5 %collective-permute-start.18 = (f32[128,16,128]{2,1,0:T(8,128)}, f32[128,16,128]{2,1,0:T(8,128)S(1)}, u32[]{:S(2)}, u32[]{:S(2)}) collective-permute-start(f32[128,16,128]{2,1,0:T(8,128)} %get-tuple-element.66), channel_id=1, source_target_pairs={{0,32},{4,64},{8,96},{12,0},{16,36},{20,68},{24,100},{28,4},{32,72... | collective-permute-start | bytes 3145736 | tf_op jit(solution)/shard_map/ppermute | solution.py:459
  88.8 86.0 %copy-start.17 = (f32[16,64,128]{2,1,0:T(8,128)S(1)}, f32[16,64,128]{2,1,0:T(8,128)}, u32[]{:S(2)}) copy-start(f32[16,64,128]{2,1,0:T(8,128)} %get-tuple-element.130) | copy-start | bytes 1572868
  88.9 86.0 %copy-start.16 = (f32[16,64,128]{2,1,0:T(8,128)S(1)}, f32[16,64,128]{2,1,0:T(8,128)}, u32[]{:S(2)}) copy-start(f32[16,64,128]{2,1,0:T(8,128)} %get-tuple-element.131) | copy-start | bytes 1572868
  88.9 86.6 %copy-start.15 = (f32[16,64,128]{2,1,0:T(8,128)S(1)}, f32[16,64,128]{2,1,0:T(8,128)}, u32[]{:S(2)}) copy-start(f32[16,64,128]{2,1,0:T(8,128)} %get-tuple-element.132) | copy-start | bytes 1572868
  88.9 91.7 %copy-start.14 = (f32[16,64,128]{2,1,0:T(8,128)S(1)}, f32[16,64,128]{2,1,0:T(8,128)}, u32[]{:S(2)}) copy-start(f32[16,64,128]{2,1,0:T(8,128)} %get-tuple-element.133) | copy-start | bytes 1572868
  88.9 31.4 %collective-permute-start.4 = (f32[16,64,128]{2,1,0:T(8,128)S(1)}, f32[16,64,128]{2,1,0:T(8,128)S(1)}, u32[]{:S(2)}, u32[]{:S(2)}) collective-permute-start(f32[16,64,128]{2,1,0:T(8,128)S(1)} %get-tuple-element.60), channel_id=1, source_target_pairs={{0,32},{4,36},{8,40},{12,44},{16,48},{20,52},{24,56},{28,60},{32,6... | collective-permute-start | bytes 1572872 | tf_op jit(solution)/shard_map/ppermute | solution.py:421
  91.3 31.0 %collective-permute-start.5 = (f32[16,64,128]{2,1,0:T(8,128)S(1)}, f32[16,64,128]{2,1,0:T(8,128)S(1)}, u32[]{:S(2)}, u32[]{:S(2)}) collective-permute-start(f32[16,64,128]{2,1,0:T(8,128)S(1)} %get-tuple-element.61), channel_id=1, source_target_pairs={{32,0},{36,4},{40,8},{44,12},{48,16},{52,20},{56,24},{60,28},{64,3... | collective-permute-start | bytes 1572872 | tf_op jit(solution)/shard_map/ppermute | solution.py:422
  92.6 35.8 %collective-permute-start.19 = (f32[128,16,128]{2,1,0:T(8,128)S(1)}, f32[128,16,128]{2,1,0:T(8,128)S(1)}, u32[]{:S(2)}, u32[]{:S(2)}) collective-permute-start(f32[128,16,128]{2,1,0:T(8,128)S(1)} %copy-done.11), channel_id=1, source_target_pairs={{0,64},{4,96},{8,0},{12,32},{16,68},{20,100},{24,4},{28,36},{32,10... | collective-permute-start | bytes 3145736 | tf_op jit(solution)/shard_map/ppermute | solution.py:459
  97.7 53.1 %collective-permute-start.20 = (f32[128,16,128]{2,1,0:T(8,128)S(1)}, f32[128,16,128]{2,1,0:T(8,128)S(1)}, u32[]{:S(2)}, u32[]{:S(2)}) collective-permute-start(f32[128,16,128]{2,1,0:T(8,128)S(1)} %copy-done.10), channel_id=1, source_target_pairs={{0,96},{4,0},{8,32},{12,64},{16,100},{20,4},{24,36},{28,68},{32,8}... | collective-permute-start | bytes 3145736 | tf_op jit(solution)/shard_map/ppermute | solution.py:459
  120.3 55.2 %collective-permute-start.6 = (f32[128,16,128]{2,1,0:T(8,128)S(1)}, f32[128,16,128]{2,1,0:T(8,128)S(1)}, u32[]{:S(2)}, u32[]{:S(2)}) collective-permute-start(f32[128,16,128]{2,1,0:T(8,128)S(1)} %get-tuple-element.62), channel_id=1, source_target_pairs={{0,4},{4,8},{8,12},{12,16},{16,20},{20,24},{24,28},{32,36},{36,40}... | collective-permute-start | bytes 3145736 | tf_op jit(solution)/shard_map/ppermute | solution.py:427
  122.2 58.3 %collective-permute-start.7 = (f32[128,16,128]{2,1,0:T(8,128)S(1)}, f32[128,16,128]{2,1,0:T(8,128)S(1)}, u32[]{:S(2)}, u32[]{:S(2)}) collective-permute-start(f32[128,16,128]{2,1,0:T(8,128)S(1)} %get-tuple-element.63), channel_id=1, source_target_pairs={{4,0},{8,4},{12,8},{16,12},{20,16},{24,20},{28,24},{36,32},{40,36}... | collective-permute-start | bytes 3145736 | tf_op jit(solution)/shard_map/ppermute | solution.py:428
  124.8 32.0 %collective-permute-start.15 = (f32[16,64,128]{2,1,0:T(8,128)S(1)}, f32[16,64,128]{2,1,0:T(8,128)S(1)}, u32[]{:S(2)}, u32[]{:S(2)}) collective-permute-start(f32[16,64,128]{2,1,0:T(8,128)S(1)} %copy-done.19), channel_id=1, source_target_pairs={{0,24},{4,28},{8,0},{12,4},{16,8},{20,12},{24,16},{28,20},{32,56},... | collective-permute-start | bytes 1572872 | tf_op jit(solution)/shard_map/ppermute | solution.py:467
  128.4 46.4 %collective-permute-start.8 = (f32[32,16,128]{2,1,0:T(8,128)S(1)}, f32[32,16,128]{2,1,0:T(8,128)S(1)}, u32[]{:S(2)}, u32[]{:S(2)}) collective-permute-start(f32[32,16,128]{2,1,0:T(8,128)S(1)} %pad_maximum_fusion.10), channel_id=1, source_target_pairs={{0,4},{4,8},{8,12},{12,16},{16,20},{20,24},{24,28},{32,36},{36,40}... | collective-permute-start | bytes 786440 | tf_op jit(solution)/shard_map/ppermute | solution.py:427
  150.8 24.1 %collective-permute-start.9 = (f32[32,16,128]{2,1,0:T(8,128)S(1)}, f32[32,16,128]{2,1,0:T(8,128)S(1)}, u32[]{:S(2)}, u32[]{:S(2)}) collective-permute-start(f32[32,16,128]{2,1,0:T(8,128)S(1)} %pad_maximum_fusion.11), channel_id=1, source_target_pairs={{4,0},{8,4},{12,8},{16,12},{20,16},{24,20},{28,24},{36,32},{40,36}... | collective-permute-start | bytes 786440 | tf_op jit(solution)/shard_map/ppermute | solution.py:428
  156.8 35.4 %collective-permute-start.14 = (f32[16,64,128]{2,1,0:T(8,128)S(1)}, f32[16,64,128]{2,1,0:T(8,128)S(1)}, u32[]{:S(2)}, u32[]{:S(2)}) collective-permute-start(f32[16,64,128]{2,1,0:T(8,128)S(1)} %copy-done.18), channel_id=1, source_target_pairs={{0,20},{4,24},{8,28},{12,0},{16,4},{20,8},{24,12},{28,16},{32,52},... | collective-permute-start | bytes 1572872 | tf_op jit(solution)/shard_map/ppermute | solution.py:467
  174.8 17.4 %collective-permute-start.13 = (f32[16,64,128]{2,1,0:T(8,128)S(1)}, f32[16,64,128]{2,1,0:T(8,128)S(1)}, u32[]{:S(2)}, u32[]{:S(2)}) collective-permute-start(f32[16,64,128]{2,1,0:T(8,128)S(1)} %copy-done.17), channel_id=1, source_target_pairs={{0,16},{4,20},{8,24},{12,28},{16,0},{20,4},{24,8},{28,12},{32,48},... | collective-permute-start | bytes 1572872 | tf_op jit(solution)/shard_map/ppermute | solution.py:467
  174.9 27.9 %collective-permute-start.12 = (f32[16,64,128]{2,1,0:T(8,128)S(1)}, f32[16,64,128]{2,1,0:T(8,128)S(1)}, u32[]{:S(2)}, u32[]{:S(2)}) collective-permute-start(f32[16,64,128]{2,1,0:T(8,128)S(1)} %copy-done.16), channel_id=1, source_target_pairs={{0,12},{4,16},{8,20},{12,24},{16,28},{20,0},{24,4},{28,8},{32,44},... | collective-permute-start | bytes 1572872 | tf_op jit(solution)/shard_map/ppermute | solution.py:467
  175.5 30.7 %collective-permute-start.11 = (f32[16,64,128]{2,1,0:T(8,128)S(1)}, f32[16,64,128]{2,1,0:T(8,128)S(1)}, u32[]{:S(2)}, u32[]{:S(2)}) collective-permute-start(f32[16,64,128]{2,1,0:T(8,128)S(1)} %copy-done.15), channel_id=1, source_target_pairs={{0,8},{4,12},{8,16},{12,20},{16,24},{20,28},{24,0},{28,4},{32,40},... | collective-permute-start | bytes 1572872 | tf_op jit(solution)/shard_map/ppermute | solution.py:467
  180.6 31.2 %collective-permute-start.10 = (f32[16,64,128]{2,1,0:T(8,128)S(1)}, f32[16,64,128]{2,1,0:T(8,128)S(1)}, u32[]{:S(2)}, u32[]{:S(2)}) collective-permute-start(f32[16,64,128]{2,1,0:T(8,128)S(1)} %copy-done.14), channel_id=1, source_target_pairs={{0,4},{4,8},{8,12},{12,16},{16,20},{20,24},{24,28},{28,0},{32,36},... | collective-permute-start | bytes 1572872 | tf_op jit(solution)/shard_map/ppermute | solution.py:467
  211.8 20.2 %collective-permute-start.25 = (f32[16,64,128]{2,1,0:T(8,128)S(1)}, f32[16,64,128]{2,1,0:T(8,128)S(1)}, u32[]{:S(2)}, u32[]{:S(2)}) collective-permute-start(f32[16,64,128]{2,1,0:T(8,128)S(1)} %get-tuple-element.85), channel_id=1, source_target_pairs={{0,32},{4,36},{8,40},{12,44},{16,48},{20,52},{24,56},{28,60},{32,6... | collective-permute-start | bytes 1572872 | tf_op jit(solution)/shard_map/ppermute | solution.py:421
  213.1 18.9 %collective-permute-start.26 = (f32[16,64,128]{2,1,0:T(8,128)S(1)}, f32[16,64,128]{2,1,0:T(8,128)S(1)}, u32[]{:S(2)}, u32[]{:S(2)}) collective-permute-start(f32[16,64,128]{2,1,0:T(8,128)S(1)} %get-tuple-element.86), channel_id=1, source_target_pairs={{32,0},{36,4},{40,8},{44,12},{48,16},{52,20},{56,24},{60,28},{64,3... | collective-permute-start | bytes 1572872 | tf_op jit(solution)/shard_map/ppermute | solution.py:422
  226.5 19.4 %collective-permute-start.21 = (f32[16,64,128]{2,1,0:T(8,128)S(1)}, f32[16,64,128]{2,1,0:T(8,128)S(1)}, u32[]{:S(2)}, u32[]{:S(2)}) collective-permute-start(f32[16,64,128]{2,1,0:T(8,128)S(1)} %get-tuple-element.80), channel_id=1, source_target_pairs={{0,32},{4,36},{8,40},{12,44},{16,48},{20,52},{24,56},{28,60},{32,6... | collective-permute-start | bytes 1572872 | tf_op jit(solution)/shard_map/ppermute | solution.py:421
  230.5 15.4 %collective-permute-start.22 = (f32[16,64,128]{2,1,0:T(8,128)S(1)}, f32[16,64,128]{2,1,0:T(8,128)S(1)}, u32[]{:S(2)}, u32[]{:S(2)}) collective-permute-start(f32[16,64,128]{2,1,0:T(8,128)S(1)} %get-tuple-element.81), channel_id=1, source_target_pairs={{32,0},{36,4},{40,8},{44,12},{48,16},{52,20},{56,24},{60,28},{64,3... | collective-permute-start | bytes 1572872 | tf_op jit(solution)/shard_map/ppermute | solution.py:422
  238.5 21.1 %collective-permute-start.27 = (f32[128,16,128]{2,1,0:T(8,128)}, f32[128,16,128]{2,1,0:T(8,128)}, u32[]{:S(2)}, u32[]{:S(2)}) collective-permute-start(f32[128,16,128]{2,1,0:T(8,128)} %get-tuple-element.88), channel_id=1, source_target_pairs={{0,4},{4,8},{8,12},{12,16},{16,20},{20,24},{24,28},{32,36},{36,40}... | collective-permute-start | bytes 3145736 | tf_op jit(solution)/shard_map/ppermute | solution.py:427
  243.5 16.4 %collective-permute-start.28 = (f32[128,16,128]{2,1,0:T(8,128)}, f32[128,16,128]{2,1,0:T(8,128)}, u32[]{:S(2)}, u32[]{:S(2)}) collective-permute-start(f32[128,16,128]{2,1,0:T(8,128)} %get-tuple-element.89), channel_id=1, source_target_pairs={{4,0},{8,4},{12,8},{16,12},{20,16},{24,20},{28,24},{36,32},{40,36}... | collective-permute-start | bytes 3145736 | tf_op jit(solution)/shard_map/ppermute | solution.py:428
  252.5 16.8 %collective-permute-start.23 = (f32[128,16,128]{2,1,0:T(8,128)}, f32[128,16,128]{2,1,0:T(8,128)}, u32[]{:S(2)}, u32[]{:S(2)}) collective-permute-start(f32[128,16,128]{2,1,0:T(8,128)} %get-tuple-element.83), channel_id=1, source_target_pairs={{0,4},{4,8},{8,12},{12,16},{16,20},{20,24},{24,28},{32,36},{36,40}... | collective-permute-start | bytes 3145736 | tf_op jit(solution)/shard_map/ppermute | solution.py:427
  256.3 16.4 %collective-permute-start.24 = (f32[128,16,128]{2,1,0:T(8,128)}, f32[128,16,128]{2,1,0:T(8,128)}, u32[]{:S(2)}, u32[]{:S(2)}) collective-permute-start(f32[128,16,128]{2,1,0:T(8,128)} %get-tuple-element.84), channel_id=1, source_target_pairs={{4,0},{8,4},{12,8},{16,12},{20,16},{24,20},{28,24},{36,32},{40,36}... | collective-permute-start | bytes 3145736 | tf_op jit(solution)/shard_map/ppermute | solution.py:428
  280.0 10.6 %collective-permute-start.29 = (f32[64,16,128]{2,1,0:T(8,128)S(1)}, f32[64,16,128]{2,1,0:T(8,128)S(1)}, u32[]{:S(2)}, u32[]{:S(2)}) collective-permute-start(f32[64,16,128]{2,1,0:T(8,128)S(1)} %get-tuple-element.123), channel_id=1, source_target_pairs={{0,1},{1,2},{2,3},{3,0},{4,5},{5,6},{6,7},{7,4},{8,9},{9,10},{10,1... | collective-permute-start | bytes 1572872 | tf_op jit(solution)/shard_map/ppermute | solution.py:407
  280.1 10.5 %collective-permute-start.31 = (f32[64,16,128]{2,1,0:T(8,128)S(1)}, f32[64,16,128]{2,1,0:T(8,128)S(1)}, u32[]{:S(2)}, u32[]{:S(2)}) collective-permute-start(f32[64,16,128]{2,1,0:T(8,128)S(1)} %get-tuple-element.124), channel_id=1, source_target_pairs={{1,0},{2,1},{3,2},{0,3},{5,4},{6,5},{7,6},{4,7},{9,8},{10,9},{11,1... | collective-permute-start | bytes 1572872 | tf_op jit(solution)/shard_map/ppermute | solution.py:408
  290.9 23.1 %collective-permute-start.32 = (f32[128,16,128]{2,1,0:T(8,128)S(1)}, f32[128,16,128]{2,1,0:T(8,128)}, u32[]{:S(2)}, u32[]{:S(2)}) collective-permute-start(f32[128,16,128]{2,1,0:T(8,128)S(1)} %pad_maximum_fusion.3), channel_id=1, source_target_pairs={{1,0},{2,1},{3,2},{0,3},{5,4},{6,5},{7,6},{4,7},{9,8},{10,9},{11,1... | collective-permute-start | bytes 3145736 | tf_op jit(solution)/shard_map/ppermute | solution.py:411
  294.9 23.8 %collective-permute-start.30 = (f32[128,16,128]{2,1,0:T(8,128)}, f32[128,16,128]{2,1,0:T(8,128)}, u32[]{:S(2)}, u32[]{:S(2)}) collective-permute-start(f32[128,16,128]{2,1,0:T(8,128)} %pad_maximum_fusion.2), channel_id=1, source_target_pairs={{0,1},{1,2},{2,3},{3,0},{4,5},{5,6},{6,7},{7,4},{8,9},{9,10},{10,1... | collective-permute-start | bytes 3145736 | tf_op jit(solution)/shard_map/ppermute | solution.py:411
  320.9 24.7 %collective-permute-start.34 = (f32[128,16,128]{2,1,0:T(8,128)S(1)}, f32[128,16,128]{2,1,0:T(8,128)S(1)}, u32[]{:S(2)}, u32[]{:S(2)}) collective-permute-start(f32[128,16,128]{2,1,0:T(8,128)S(1)} %fusion.9.refs_0_), channel_id=1, source_target_pairs={{0,1},{1,2},{2,3},{3,0},{4,5},{5,6},{6,7},{7,4},{8,9},{9,10},{10,1... | collective-permute-start | bytes 3145736 | tf_op jit(solution)/shard_map/ppermute | solution.py:398
  321.0 24.7 %collective-permute-start.33 = (f32[128,16,128]{2,1,0:T(8,128)S(1)}, f32[128,16,128]{2,1,0:T(8,128)S(1)}, u32[]{:S(2)}, u32[]{:S(2)}) collective-permute-start(f32[128,16,128]{2,1,0:T(8,128)S(1)} %fusion.9.refs_0_), channel_id=1, source_target_pairs={{1,0},{2,1},{3,2},{0,3},{5,4},{6,5},{7,6},{4,7},{9,8},{10,9},{11,1... | collective-permute-start | bytes 3145736 | tf_op jit(solution)/shard_map/ppermute | solution.py:399
  345.6 14.6 %collective-permute-start.35 = (f32[64,16,128]{2,1,0:T(8,128)S(1)}, f32[64,16,128]{2,1,0:T(8,128)S(1)}, u32[]{:S(2)}, u32[]{:S(2)}) collective-permute-start(f32[64,16,128]{2,1,0:T(8,128)S(1)} %slice.238), channel_id=1, source_target_pairs={{0,1},{1,2},{2,3},{3,0},{4,5},{5,6},{6,7},{7,4},{8,9},{9,10},{10,1... | collective-permute-start | bytes 1572872 | tf_op jit(solution)/shard_map/ppermute | solution.py:400
  345.8 14.9 %collective-permute-start.36 = (f32[64,16,128]{2,1,0:T(8,128)S(1)}, f32[64,16,128]{2,1,0:T(8,128)S(1)}, u32[]{:S(2)}, u32[]{:S(2)}) collective-permute-start(f32[64,16,128]{2,1,0:T(8,128)S(1)} %slice.239), channel_id=1, source_target_pairs={{1,0},{2,1},{3,2},{0,3},{5,4},{6,5},{7,6},{4,7},{9,8},{10,9},{11,1... | collective-permute-start | bytes 1572872 | tf_op jit(solution)/shard_map/ppermute | solution.py:401
  362.3 16.1 %collective-permute-start.37 = (f32[16,64,128]{2,1,0:T(8,128)S(1)}, f32[16,64,128]{2,1,0:T(8,128)S(1)}, u32[]{:S(2)}, u32[]{:S(2)}) collective-permute-start(f32[16,64,128]{2,1,0:T(8,128)S(1)} %get-tuple-element.91), channel_id=1, source_target_pairs={{0,32},{4,36},{8,40},{12,44},{16,48},{20,52},{24,56},{28,60},{32,6... | collective-permute-start | bytes 1572872 | tf_op jit(solution)/shard_map/ppermute | solution.py:421
  367.8 14.8 %collective-permute-start.38 = (f32[16,64,128]{2,1,0:T(8,128)S(1)}, f32[16,64,128]{2,1,0:T(8,128)S(1)}, u32[]{:S(2)}, u32[]{:S(2)}) collective-permute-start(f32[16,64,128]{2,1,0:T(8,128)S(1)} %get-tuple-element.92), channel_id=1, source_target_pairs={{32,0},{36,4},{40,8},{44,12},{48,16},{52,20},{56,24},{60,28},{64,3... | collective-permute-start | bytes 1572872 | tf_op jit(solution)/shard_map/ppermute | solution.py:422
  369.1 28.0 %collective-permute-start.39 = (f32[128,16,128]{2,1,0:T(8,128)S(1)}, f32[128,16,128]{2,1,0:T(8,128)S(1)}, u32[]{:S(2)}, u32[]{:S(2)}) collective-permute-start(f32[128,16,128]{2,1,0:T(8,128)S(1)} %get-tuple-element.93), channel_id=1, source_target_pairs={{0,4},{4,8},{8,12},{12,16},{16,20},{20,24},{24,28},{32,36},{36,40}... | collective-permute-start | bytes 3145736 | tf_op jit(solution)/shard_map/ppermute | solution.py:427
  376.5 20.7 %collective-permute-start.40 = (f32[128,16,128]{2,1,0:T(8,128)S(1)}, f32[128,16,128]{2,1,0:T(8,128)S(1)}, u32[]{:S(2)}, u32[]{:S(2)}) collective-permute-start(f32[128,16,128]{2,1,0:T(8,128)S(1)} %get-tuple-element.94), channel_id=1, source_target_pairs={{4,0},{8,4},{12,8},{16,12},{20,16},{24,20},{28,24},{36,32},{40,36}... | collective-permute-start | bytes 3145736 | tf_op jit(solution)/shard_map/ppermute | solution.py:428
  382.7 10.0 %collective-permute-start.41 = (f32[32,16,128]{2,1,0:T(8,128)S(1)}, f32[32,16,128]{2,1,0:T(8,128)S(1)}, u32[]{:S(2)}, u32[]{:S(2)}) collective-permute-start(f32[32,16,128]{2,1,0:T(8,128)S(1)} %pad_maximum_fusion.12), channel_id=1, source_target_pairs={{0,4},{4,8},{8,12},{12,16},{16,20},{20,24},{24,28},{32,36},{36,40}... | collective-permute-start | bytes 786440 | tf_op jit(solution)/shard_map/ppermute | solution.py:427
  389.5 7.7 %collective-permute-start.42 = (f32[32,16,128]{2,1,0:T(8,128)S(1)}, f32[32,16,128]{2,1,0:T(8,128)S(1)}, u32[]{:S(2)}, u32[]{:S(2)}) collective-permute-start(f32[32,16,128]{2,1,0:T(8,128)S(1)} %pad_maximum_fusion.13), channel_id=1, source_target_pairs={{4,0},{8,4},{12,8},{16,12},{20,16},{24,20},{28,24},{36,32},{40,36}... | collective-permute-start | bytes 786440 | tf_op jit(solution)/shard_map/ppermute | solution.py:428
  407.8 20.7 %collective-permute-start.47 = (f32[16,64,128]{2,1,0:T(8,128)S(1)}, f32[16,64,128]{2,1,0:T(8,128)S(1)}, u32[]{:S(2)}, u32[]{:S(2)}) collective-permute-start(f32[16,64,128]{2,1,0:T(8,128)S(1)} %get-tuple-element.102), channel_id=1, source_target_pairs={{0,32},{4,36},{8,40},{12,44},{16,48},{20,52},{24,56},{28,60},{32,6... | collective-permute-start | bytes 1572872 | tf_op jit(solution)/shard_map/ppermute | solution.py:421
  411.2 17.3 %collective-permute-start.48 = (f32[16,64,128]{2,1,0:T(8,128)S(1)}, f32[16,64,128]{2,1,0:T(8,128)S(1)}, u32[]{:S(2)}, u32[]{:S(2)}) collective-permute-start(f32[16,64,128]{2,1,0:T(8,128)S(1)} %get-tuple-element.103), channel_id=1, source_target_pairs={{32,0},{36,4},{40,8},{44,12},{48,16},{52,20},{56,24},{60,28},{64,3... | collective-permute-start | bytes 1572872 | tf_op jit(solution)/shard_map/ppermute | solution.py:422
  423.1 13.0 %collective-permute-start.43 = (f32[16,64,128]{2,1,0:T(8,128)S(1)}, f32[16,64,128]{2,1,0:T(8,128)S(1)}, u32[]{:S(2)}, u32[]{:S(2)}) collective-permute-start(f32[16,64,128]{2,1,0:T(8,128)S(1)} %get-tuple-element.96), channel_id=1, source_target_pairs={{0,32},{4,36},{8,40},{12,44},{16,48},{20,52},{24,56},{28,60},{32,6... | collective-permute-start | bytes 1572872 | tf_op jit(solution)/shard_map/ppermute | solution.py:421
  427.2 12.6 %collective-permute-start.44 = (f32[16,64,128]{2,1,0:T(8,128)S(1)}, f32[16,64,128]{2,1,0:T(8,128)S(1)}, u32[]{:S(2)}, u32[]{:S(2)}) collective-permute-start(f32[16,64,128]{2,1,0:T(8,128)S(1)} %get-tuple-element.97), channel_id=1, source_target_pairs={{32,0},{36,4},{40,8},{44,12},{48,16},{52,20},{56,24},{60,28},{64,3... | collective-permute-start | bytes 1572872 | tf_op jit(solution)/shard_map/ppermute | solution.py:422
  431.6 17.5 %collective-permute-start.49 = (f32[128,16,128]{2,1,0:T(8,128)S(1)}, f32[128,16,128]{2,1,0:T(8,128)S(1)}, u32[]{:S(2)}, u32[]{:S(2)}) collective-permute-start(f32[128,16,128]{2,1,0:T(8,128)S(1)} %get-tuple-element.105), channel_id=1, source_target_pairs={{0,4},{4,8},{8,12},{12,16},{16,20},{20,24},{24,28},{32,36},{36,40}... | collective-permute-start | bytes 3145736 | tf_op jit(solution)/shard_map/ppermute | solution.py:427
  434.2 16.1 %collective-permute-start.50 = (f32[128,16,128]{2,1,0:T(8,128)S(1)}, f32[128,16,128]{2,1,0:T(8,128)S(1)}, u32[]{:S(2)}, u32[]{:S(2)}) collective-permute-start(f32[128,16,128]{2,1,0:T(8,128)S(1)} %get-tuple-element.106), channel_id=1, source_target_pairs={{4,0},{8,4},{12,8},{16,12},{20,16},{24,20},{28,24},{36,32},{40,36}... | collective-permute-start | bytes 3145736 | tf_op jit(solution)/shard_map/ppermute | solution.py:428
  442.9 16.0 %collective-permute-start.45 = (f32[128,16,128]{2,1,0:T(8,128)S(1)}, f32[128,16,128]{2,1,0:T(8,128)S(1)}, u32[]{:S(2)}, u32[]{:S(2)}) collective-permute-start(f32[128,16,128]{2,1,0:T(8,128)S(1)} %get-tuple-element.99), channel_id=1, source_target_pairs={{0,4},{4,8},{8,12},{12,16},{16,20},{20,24},{24,28},{32,36},{36,40}... | collective-permute-start | bytes 3145736 | tf_op jit(solution)/shard_map/ppermute | solution.py:427
  447.2 16.4 %collective-permute-start.46 = (f32[128,16,128]{2,1,0:T(8,128)S(1)}, f32[128,16,128]{2,1,0:T(8,128)S(1)}, u32[]{:S(2)}, u32[]{:S(2)}) collective-permute-start(f32[128,16,128]{2,1,0:T(8,128)S(1)} %get-tuple-element.100), channel_id=1, source_target_pairs={{4,0},{8,4},{12,8},{16,12},{20,16},{24,20},{28,24},{36,32},{40,36}... | collective-permute-start | bytes 3145736 | tf_op jit(solution)/shard_map/ppermute | solution.py:428
  469.8 12.2 %collective-permute-start.51 = (f32[64,16,128]{2,1,0:T(8,128)S(1)}, f32[64,16,128]{2,1,0:T(8,128)S(1)}, u32[]{:S(2)}, u32[]{:S(2)}) collective-permute-start(f32[64,16,128]{2,1,0:T(8,128)S(1)} %get-tuple-element.117), channel_id=1, source_target_pairs={{0,1},{1,2},{2,3},{3,0},{4,5},{5,6},{6,7},{7,4},{8,9},{9,10},{10,1... | collective-permute-start | bytes 1572872 | tf_op jit(solution)/shard_map/ppermute | solution.py:407
  469.9 14.6 %collective-permute-start.53 = (f32[64,16,128]{2,1,0:T(8,128)S(1)}, f32[64,16,128]{2,1,0:T(8,128)S(1)}, u32[]{:S(2)}, u32[]{:S(2)}) collective-permute-start(f32[64,16,128]{2,1,0:T(8,128)S(1)} %get-tuple-element.118), channel_id=1, source_target_pairs={{1,0},{2,1},{3,2},{0,3},{5,4},{6,5},{7,6},{4,7},{9,8},{10,9},{11,1... | collective-permute-start | bytes 1572872 | tf_op jit(solution)/shard_map/ppermute | solution.py:408
  484.8 16.8 %collective-permute-start.54 = (f32[128,16,128]{2,1,0:T(8,128)S(1)}, f32[128,16,128]{2,1,0:T(8,128)S(1)}, u32[]{:S(2)}, u32[]{:S(2)}) collective-permute-start(f32[128,16,128]{2,1,0:T(8,128)S(1)} %pad_maximum_fusion.6), channel_id=1, source_target_pairs={{1,0},{2,1},{3,2},{0,3},{5,4},{6,5},{7,6},{4,7},{9,8},{10,9},{11,1... | collective-permute-start | bytes 3145736 | tf_op jit(solution)/shard_map/ppermute | solution.py:411
  488.3 14.9 %collective-permute-start.52 = (f32[128,16,128]{2,1,0:T(8,128)S(1)}, f32[128,16,128]{2,1,0:T(8,128)S(1)}, u32[]{:S(2)}, u32[]{:S(2)}) collective-permute-start(f32[128,16,128]{2,1,0:T(8,128)S(1)} %pad_maximum_fusion.5), channel_id=1, source_target_pairs={{0,1},{1,2},{2,3},{3,0},{4,5},{5,6},{6,7},{7,4},{8,9},{9,10},{10,1... | collective-permute-start | bytes 3145736 | tf_op jit(solution)/shard_map/ppermute | solution.py:411
  526.9 25.0 %collective-permute-start.56 = (f32[16,128,128]{2,1,0:T(8,128)S(1)}, f32[16,128,128]{2,1,0:T(8,128)S(1)}, u32[]{:S(2)}, u32[]{:S(2)}) collective-permute-start(f32[16,128,128]{2,1,0:T(8,128)S(1)} %bitcast.160), channel_id=1, source_target_pairs={{0,1},{1,2},{2,3},{3,0},{4,5},{5,6},{6,7},{7,4},{8,9},{9,10},{10,1... | collective-permute-start | bytes 3145736 | tf_op jit(solution)/shard_map/ppermute | solution.py:398
  527.0 25.0 %collective-permute-start.55 = (f32[16,128,128]{2,1,0:T(8,128)S(1)}, f32[16,128,128]{2,1,0:T(8,128)S(1)}, u32[]{:S(2)}, u32[]{:S(2)}) collective-permute-start(f32[16,128,128]{2,1,0:T(8,128)S(1)} %bitcast.161), channel_id=1, source_target_pairs={{1,0},{2,1},{3,2},{0,3},{5,4},{6,5},{7,6},{4,7},{9,8},{10,9},{11,1... | collective-permute-start | bytes 3145736 | tf_op jit(solution)/shard_map/ppermute | solution.py:399
  551.9 12.9 %collective-permute-start.57 = (f32[8,128,128]{2,1,0:T(8,128)S(1)}, f32[8,128,128]{2,1,0:T(8,128)S(1)}, u32[]{:S(2)}, u32[]{:S(2)}) collective-permute-start(f32[8,128,128]{2,1,0:T(8,128)S(1)} %slice.251), channel_id=1, source_target_pairs={{0,1},{1,2},{2,3},{3,0},{4,5},{5,6},{6,7},{7,4},{8,9},{9,10},{10,1... | collective-permute-start | bytes 1572872 | tf_op jit(solution)/shard_map/ppermute | solution.py:400
  552.1 12.7 %collective-permute-start.58 = (f32[8,128,128]{2,1,0:T(8,128)S(1)}, f32[8,128,128]{2,1,0:T(8,128)S(1)}, u32[]{:S(2)}, u32[]{:S(2)}) collective-permute-start(f32[8,128,128]{2,1,0:T(8,128)S(1)} %slice.252), channel_id=1, source_target_pairs={{1,0},{2,1},{3,2},{0,3},{5,4},{6,5},{7,6},{4,7},{9,8},{10,9},{11,1... | collective-permute-start | bytes 1572872 | tf_op jit(solution)/shard_map/ppermute | solution.py:401
  (25 other events, 458.5 us)
